TPU v7x, 512 devices: a whole 4x8x8 slice. The times are simulated.
512 devices in a mesh: dp: 16 (over y, core), expert: 32 (over x, z).
Axes of the slice: x: 4, y: 8, z: 8, core: 2. Of those that a mesh axis runs over, the one named last changes fastest.
Arguments:
- tokens: bfloat16 [2, 8192, 3584], P(None, ('dp', 'expert')), parts along dimension 1, may hold values from -6 to 6
- expert_ids: int32 [2, 8192, 2], P(None, ('dp', 'expert')), parts along dimension 1, may hold values from 0 to 3, as said below
- route_weights: float32 [2, 8192, 2], P(None, ('dp', 'expert')), parts along dimension 1, may hold values from 0.4 to 2
- owner_map: int32 [64], P('dp'), parts along dimension 0, may hold values from 0 to 3, each once
- expert_weights: bfloat16 [4096, 3, 3584], P('expert'), may hold values from -0.09375 to 0.09375
Outputs:
- mixed: bfloat16 [2, 8192, 3584], P(None, ('dp', 'expert')), parts along dimension 1
There are 16 independent parts, one for each index of `dp`. A program takes and returns all parts, laid end to end along the dimension named above; an argument that names none is the same for every part. Nothing has to cross between parts.
Inputs may be any that keep to these rules, and one draw needn't show every extreme that they name: `expert_ids`: each token names 2 different experts. One expert, the same for all steps and devices of a part, is named by at least 8 of the tokens of every device in every step, by all 16 tokens of some device in some step, and by more of the tokens of every device over the 2 steps together than any other expert; every other expert is named by at most 8 tokens of one device in one step, a bound reached in every draw. `owner_map`: each group owns exactly one expert.
All inputs are finite; a program needn't handle non-finite values.
Results may differ from a plain program's by a relative error of at most 0.006.
Values may be sent and summed in bfloat16 or wider, within the bound.
No kernel may reach another device: no remote copies, remote signals or barrier semaphores. Data moves between devices by JAX's collectives and lax.ppermute only.
A program may use at most 64 MiB of HBM per device.

v0:
```python
import jax
import jax.numpy as jnp
from jax import lax
from jax.sharding import Mesh, PartitionSpec as P


EXPERTS = 4
ROWS = 32
AXES = ("y", "core", "x", "z")


def from_offset(block, axis, offset):
    size = lax.axis_size(axis)
    return lax.ppermute(block, axis, [((i + offset) % size, i) for i in range(size)])


def narrow(values):
    return lax.reduce_precision(values, 8, 7)


def packed_tokens(tokens, expert_ids, route_weights, owner_map):
    rows = tokens.shape[0] * tokens.shape[1]
    groups = jnp.arange(EXPERTS)
    group = jnp.sum(jnp.where(expert_ids[..., None] == groups, owner_map, 0), axis=-1)
    coef = jnp.sum(
        jnp.where(group[..., None] == groups, route_weights[..., None], 0.0), axis=2
    ).reshape(rows, EXPERTS)
    high = narrow(coef)
    middle = narrow(coef - high)
    low = coef - high - middle
    tail = jnp.concatenate([high, middle, low, jnp.zeros((rows, 116), jnp.float32)], axis=1)
    return jnp.concatenate([tokens.reshape(rows, -1), tail.astype(jnp.bfloat16)], axis=1)


def gathered_tokens(own):
    up2 = from_offset(own, "z", 2)
    down2 = from_offset(own, "z", -2)
    far = from_offset(own, "z", 4)
    up13 = from_offset(jnp.concatenate([own, up2]), "z", 1)
    down13 = from_offset(jnp.concatenate([own, down2]), "z", -1)
    return jnp.concatenate([own, up13, down13, up2, down2, far])


def gate_up_pieces(weights, start):
    width = weights.shape[2]
    sent = lax.dynamic_slice(weights, (start, 0, 0), (32, 2, width)).transpose(1, 0, 2)
    arrived = [from_offset(sent, "x", k) for k in (1, 3, 2)]
    three = jnp.stack(arrived, axis=1).reshape(2, 96, width)
    gate, up = three[0], three[1]
    more = [from_offset(gate, "y", -1), from_offset(up, "y", 1)]
    half = jnp.stack([three, jnp.stack(more)], axis=1).reshape(384, width)
    return half, from_offset(half, "core", 1)


def down_pieces(weights, start, rest):
    width = weights.shape[2]
    sent = jnp.stack(
        [lax.dynamic_slice(weights, (row, 2, 0), (32, 1, width)).reshape(32, width) for row in (start, rest)]
    )
    arrived = [from_offset(sent, "x", k) for k in (1, 3, 2)]
    half = jnp.stack(arrived, axis=1).reshape(192, width)
    return half, from_offset(half, "core", 1)


def dot_t(a, b):
    return lax.dot_general(a, b, (((1,), (1,)), ((), ())), preferred_element_type=jnp.float32)


def coefficients(x_index, tail):
    position = jnp.arange(512)
    third = position // 32 % 3
    offset = jnp.where(position < 128, 0, jnp.where(third == 1, 1, jnp.where(third == 2, 3, 2)))
    group = (x_index + offset) % EXPERTS
    column = jnp.arange(128)
    chosen = (column < 3 * EXPERTS) & (column % EXPERTS == group[:, None])
    return dot_t(chosen.astype(jnp.bfloat16), tail)


def hidden_units(coef, tokens, own, half, other):
    first, second, third = dot_t(own, tokens), dot_t(half, tokens), dot_t(other, tokens)
    gate = jnp.concatenate([first[:128], second[:192], third[:192]])
    up = jnp.concatenate([first[128:], second[192:], third[192:]])
    hidden = narrow(gate / (1.0 + jnp.exp(-gate)) * up)
    return (hidden * coef).astype(jnp.bfloat16)


def returned(hidden, own, half, other):
    rows = jnp.concatenate([own, half, other])
    part = lax.dot_general(hidden, rows, (((0,), (0,)), ((), ())), preferred_element_type=jnp.float32)
    keep, up1, up3, down1, down3, up2, down2, far = part.astype(jnp.bfloat16).reshape(8, ROWS, -1)
    even = lax.axis_index("z") % 2 == 0
    wide = lambda v: v.astype(jnp.float32)
    pairs = [(i, (i + 2) % 8 if i % 2 == 0 else (i - 2) % 8) for i in range(8)]
    far = wide(lax.ppermute(far, "z", pairs))
    from_up3 = from_offset(down3, "z", 1)
    from_down3 = from_offset(up3, "z", -1)
    from_up1 = from_offset(down1, "z", 1)
    from_down1 = from_offset(up1, "z", -1)
    sum_up2 = wide(up2) + wide(from_down3) + jnp.where(even, far, 0.0)
    sum_down2 = wide(down2) + wide(from_up3) + jnp.where(even, 0.0, far)
    from_up2 = from_offset(sum_down2.astype(jnp.bfloat16), "z", 2)
    from_down2 = from_offset(sum_up2.astype(jnp.bfloat16), "z", -2)
    return (wide(keep) + wide(from_down1) + wide(from_up1)
            + wide(from_down2) + wide(from_up2)).astype(jnp.bfloat16)


def shards(tokens, expert_ids, route_weights, owner_map, expert_weights):
    width = tokens.shape[-1]
    core, parity, x_index = lax.axis_index("core"), lax.axis_index("y") % 2, lax.axis_index("x")
    start, rest = core * 64 + parity * 32, core * 64 + 32 - parity * 32
    packed = packed_tokens(tokens, expert_ids, route_weights, owner_map)
    planes = expert_weights.transpose(1, 0, 2)
    half, other = gate_up_pieces(expert_weights, start)
    down_half, down_other = down_pieces(expert_weights, start, rest)
    gathered = gathered_tokens(packed)
    coef = coefficients(x_index, gathered[:, width:])
    own = planes[:2].reshape(256, width)
    hidden = hidden_units(coef, gathered[:, :width], own, half, other)
    return returned(hidden, planes[2], down_half, down_other).reshape(tokens.shape)


def solution(mesh):
    split = Mesh(mesh.devices.reshape(8, 2, 4, 8), AXES)
    rows = P(None, AXES, None)
    return jax.shard_map(
        shards,
        mesh=split,
        in_specs=(rows, rows, rows, P(AXES[:2]), P(AXES[2:], None, None)),
        out_specs=rows,
        check_vma=False,
    )
```

profile of v0, /device:TPU:26, one launch (start us, length us, event | category | flops | bytes accessed | tf_op | source)
XLA Modules:
  0.0 139.9 jit_solution(6852927109695105845)
XLA Ops:
  0.0 2.0 %dynamic-slice_bitcast_fusion = bf16[2,32,3584]{2,1,0:T(8,128)(2,1)} fusion(bf16[128,3,3584]{2,0,1:T(8,128)(2,1)} %param.9, s32[]{:T(128)S(6)} %select_n.103), kind=kLoop, calls=%fused_computation.41 | loop fusion | bytes 917508 | tf_op jit(solution)/shard_map/transpose | solution.py:46
  2.0 2.4 %collective-permute-start.5 = (bf16[2,32,3584]{2,1,0:T(8,128)(2,1)}, bf16[2,32,3584]{2,1,0:T(8,128)(2,1)}, u32[]{:S(2)}, u32[]{:S(2)}) collective-permute-start(bf16[2,32,3584]{2,1,0:T(8,128)(2,1)} %dynamic-slice_bitcast_fusion), channel_id=1, source_target_pairs={{8,0},{16,8},{24,16},{0,24},{9,1},{17,9},{25,17},{1,25},{10,2},{18... | collective-permute-start | bytes 1376264 | tf_op jit(solution)/shard_map/ppermute | solution.py:14
  4.4 3.4 %collective-permute-start.6 = (bf16[2,32,3584]{2,1,0:T(8,128)(2,1)}, bf16[2,32,3584]{2,1,0:T(8,128)(2,1)}, u32[]{:S(2)}, u32[]{:S(2)}) collective-permute-start(bf16[2,32,3584]{2,1,0:T(8,128)(2,1)} %dynamic-slice_bitcast_fusion), channel_id=1, source_target_pairs={{24,0},{0,8},{8,16},{16,24},{25,1},{1,9},{9,17},{17,25},{26,2},{2,... | collective-permute-start | bytes 1376264 | tf_op jit(solution)/shard_map/ppermute | solution.py:14
  7.8 5.2 %collective-permute-start.7 = (bf16[2,32,3584]{2,1,0:T(8,128)(2,1)}, bf16[2,32,3584]{2,1,0:T(8,128)(2,1)}, u32[]{:S(2)}, u32[]{:S(2)}) collective-permute-start(bf16[2,32,3584]{2,1,0:T(8,128)(2,1)} %dynamic-slice_bitcast_fusion), channel_id=1, source_target_pairs={{16,0},{24,8},{0,16},{8,24},{17,1},{25,9},{1,17},{9,25},{18,2},{26... | collective-permute-start | bytes 1376264 | tf_op jit(solution)/shard_map/ppermute | solution.py:14
  16.0 10.9 %collective-permute-start = (bf16[32,3712]{1,0:T(8,128)(2,1)S(1)}, bf16[32,3712]{1,0:T(8,128)(2,1)S(1)}, u32[]{:S(2)}, u32[]{:S(2)}) collective-permute-start(bf16[32,3712]{1,0:T(8,128)(2,1)S(1)} %concatenate.24), channel_id=1, source_target_pairs={{2,0},{3,1},{4,2},{5,3},{6,4},{7,5},{0,6},{1,7},{10,8},{11,9},{12,... | collective-permute-start | bytes 712712 | tf_op jit(solution)/shard_map/ppermute | solution.py:14
  26.9 1.9 %collective-permute-start.2 = (bf16[32,3712]{1,0:T(8,128)(2,1)S(1)}, bf16[32,3712]{1,0:T(8,128)(2,1)S(1)}, u32[]{:S(2)}, u32[]{:S(2)}) collective-permute-start(bf16[32,3712]{1,0:T(8,128)(2,1)S(1)} %concatenate.24), channel_id=1, source_target_pairs={{6,0},{7,1},{0,2},{1,3},{2,4},{3,5},{4,6},{5,7},{14,8},{15,9},{8,1... | collective-permute-start | bytes 712712 | tf_op jit(solution)/shard_map/ppermute | solution.py:14
  33.9 2.3 %collective-permute-done = bf16[32,3712]{1,0:T(8,128)(2,1)S(1)} collective-permute-done((bf16[32,3712]{1,0:T(8,128)(2,1)S(1)}, bf16[32,3712]{1,0:T(8,128)(2,1)S(1)}, u32[]{:S(2)}, u32[]{:S(2)}) %collective-permute-start) | collective-permute-done | bytes 237600 | tf_op jit(solution)/shard_map/ppermute | solution.py:14
  36.2 5.3 %collective-permute-start.4 = (bf16[32,3712]{1,0:T(8,128)(2,1)S(1)}, bf16[32,3712]{1,0:T(8,128)(2,1)S(1)}, u32[]{:S(2)}, u32[]{:S(2)}) collective-permute-start(bf16[32,3712]{1,0:T(8,128)(2,1)S(1)} %concatenate.24), channel_id=1, source_target_pairs={{4,0},{5,1},{6,2},{7,3},{0,4},{1,5},{2,6},{3,7},{12,8},{13,9},{14,... | collective-permute-start | bytes 712712 | tf_op jit(solution)/shard_map/ppermute | solution.py:14
  42.4 2.1 %collective-permute-start.11 = (bf16[2,32,3584]{2,1,0:T(8,128)(2,1)}, bf16[2,32,3584]{2,1,0:T(8,128)(2,1)S(1)}, u32[]{:S(2)}, u32[]{:S(2)}) collective-permute-start(bf16[2,32,3584]{2,1,0:T(8,128)(2,1)} %pad_maximum_fusion.7), channel_id=1, source_target_pairs={{8,0},{16,8},{24,16},{0,24},{9,1},{17,9},{25,17},{1,25},{10,2},{18... | collective-permute-start | bytes 1376264 | tf_op jit(solution)/shard_map/ppermute | solution.py:14
  44.7 3.7 %collective-permute-start.12 = (bf16[2,32,3584]{2,1,0:T(8,128)(2,1)}, bf16[2,32,3584]{2,1,0:T(8,128)(2,1)S(1)}, u32[]{:S(2)}, u32[]{:S(2)}) collective-permute-start(bf16[2,32,3584]{2,1,0:T(8,128)(2,1)} %pad_maximum_fusion.7), channel_id=1, source_target_pairs={{24,0},{0,8},{8,16},{16,24},{25,1},{1,9},{9,17},{17,25},{26,2},{2,... | collective-permute-start | bytes 1376264 | tf_op jit(solution)/shard_map/ppermute | solution.py:14
  48.4 3.4 %collective-permute-start.13 = (bf16[2,32,3584]{2,1,0:T(8,128)(2,1)}, bf16[2,32,3584]{2,1,0:T(8,128)(2,1)S(1)}, u32[]{:S(2)}, u32[]{:S(2)}) collective-permute-start(bf16[2,32,3584]{2,1,0:T(8,128)(2,1)} %pad_maximum_fusion.7), channel_id=1, source_target_pairs={{16,0},{24,8},{0,16},{8,24},{17,1},{25,9},{1,17},{9,25},{18,2},{26... | collective-permute-start | bytes 1376264 | tf_op jit(solution)/shard_map/ppermute | solution.py:14
  51.8 1.9 %collective-permute-start.1 = (bf16[64,3712]{1,0:T(8,128)(2,1)S(1)}, bf16[64,3712]{1,0:T(8,128)(2,1)S(1)}, u32[]{:S(2)}, u32[]{:S(2)}) collective-permute-start(bf16[64,3712]{1,0:T(8,128)(2,1)S(1)} %get-tuple-element.23), channel_id=1, source_target_pairs={{1,0},{2,1},{3,2},{4,3},{5,4},{6,5},{7,6},{0,7},{9,8},{10,9},{11,1... | collective-permute-start | bytes 1425416 | tf_op jit(solution)/shard_map/ppermute | solution.py:14
  53.7 1.5 %pad_maximum_fusion.1 = bf16[2,3,32,3584]{3,2,1,0:T(8,128)(2,1)S(1)} fusion(bf16[2,1,32,3584]{3,2,1,0:T(8,128)(2,1)} %bitcast.9, bf16[2,1,32,3584]{3,2,1,0:T(8,128)(2,1)} %bitcast.8, bf16[2,1,32,3584]{3,2,1,0:T(8,128)(2,1)} %bitcast.6), kind=kLoop, calls=%fused_computation.13 | loop fusion | flops 1376256 | bytes 2752512 | tf_op jit(solution)/shard_map/stack | solution.py:48
  55.3 8.4 %collective-permute-done.11 = bf16[2,32,3584]{2,1,0:T(8,128)(2,1)S(1)} collective-permute-done((bf16[2,32,3584]{2,1,0:T(8,128)(2,1)}, bf16[2,32,3584]{2,1,0:T(8,128)(2,1)S(1)}, u32[]{:S(2)}, u32[]{:S(2)}) %collective-permute-start.11) | collective-permute-done | bytes 458784 | tf_op jit(solution)/shard_map/ppermute | solution.py:14
  63.7 5.4 %collective-permute-start.3 = (bf16[64,3712]{1,0:T(8,128)(2,1)S(1)}, bf16[64,3712]{1,0:T(8,128)(2,1)S(1)}, u32[]{:S(2)}, u32[]{:S(2)}) collective-permute-start(bf16[64,3712]{1,0:T(8,128)(2,1)S(1)} %get-tuple-element.22), channel_id=1, source_target_pairs={{7,0},{0,1},{1,2},{2,3},{3,4},{4,5},{5,6},{6,7},{15,8},{8,9},{9,10... | collective-permute-start | bytes 1425416 | tf_op jit(solution)/shard_map/ppermute | solution.py:14
  69.1 4.7 %collective-permute-start.8 = (bf16[96,3584]{1,0:T(8,128)(2,1)S(1)}, bf16[96,3584]{1,0:T(8,128)(2,1)S(1)}, u32[]{:S(2)}, u32[]{:S(2)}) collective-permute-start(bf16[96,3584]{1,0:T(8,128)(2,1)S(1)} %bitcast.51), channel_id=1, source_target_pairs={{448,0},{0,64},{64,128},{128,192},{192,256},{256,320},{320,384},{3... | collective-permute-start | bytes 2064392 | tf_op jit(solution)/shard_map/ppermute | solution.py:14
  73.8 1.9 %collective-permute-start.9 = (bf16[96,3584]{1,0:T(8,128)(2,1)S(1)}, bf16[96,3584]{1,0:T(8,128)(2,1)S(1)}, u32[]{:S(2)}, u32[]{:S(2)}) collective-permute-start(bf16[96,3584]{1,0:T(8,128)(2,1)S(1)} %bitcast.50), channel_id=1, source_target_pairs={{64,0},{128,64},{192,128},{256,192},{320,256},{384,320},{448,384},... | collective-permute-start | bytes 2064392 | tf_op jit(solution)/shard_map/ppermute | solution.py:14
  75.9 1.9 %collective-permute-start.14 = (bf16[192,3584]{1,0:T(8,128)(2,1)S(1)}, bf16[192,3584]{1,0:T(8,128)(2,1)S(1)}, u32[]{:S(2)}, u32[]{:S(2)}) collective-permute-start(bf16[192,3584]{1,0:T(8,128)(2,1)S(1)} %bitcast.48), channel_id=1, source_target_pairs={{32,0},{0,32},{33,1},{1,33},{34,2},{2,34},{35,3},{3,35},{36,4},{4,... | collective-permute-start | bytes 4128776 | tf_op jit(solution)/shard_map/ppermute | solution.py:14
  77.9 4.3 %collective-permute-done.8 = bf16[96,3584]{1,0:T(8,128)(2,1)S(1)} collective-permute-done((bf16[96,3584]{1,0:T(8,128)(2,1)S(1)}, bf16[96,3584]{1,0:T(8,128)(2,1)S(1)}, u32[]{:S(2)}, u32[]{:S(2)}) %collective-permute-start.8) | collective-permute-done | bytes 688160 | tf_op jit(solution)/shard_map/ppermute | solution.py:14
  82.2 5.6 %collective-permute-done.9 = bf16[96,3584]{1,0:T(8,128)(2,1)S(1)} collective-permute-done((bf16[96,3584]{1,0:T(8,128)(2,1)S(1)}, bf16[96,3584]{1,0:T(8,128)(2,1)S(1)}, u32[]{:S(2)}, u32[]{:S(2)}) %collective-permute-start.9) | collective-permute-done | bytes 688160 | tf_op jit(solution)/shard_map/ppermute | solution.py:14
  88.5 2.1 %collective-permute-start.10 = (bf16[384,3584]{1,0:T(8,128)(2,1)S(1)}, bf16[384,3584]{1,0:T(8,128)(2,1)S(1)}, u32[]{:S(2)}, u32[]{:S(2)}) collective-permute-start(bf16[384,3584]{1,0:T(8,128)(2,1)S(1)} %bitcast.45), channel_id=1, source_target_pairs={{32,0},{0,32},{33,1},{1,33},{34,2},{2,34},{35,3},{3,35},{36,4},{4,... | collective-permute-start | bytes 8257544 | tf_op jit(solution)/shard_map/ppermute | solution.py:14
  93.7 1.9 %collective-permute-done.10 = bf16[384,3584]{1,0:T(8,128)(2,1)S(1)} collective-permute-done((bf16[384,3584]{1,0:T(8,128)(2,1)S(1)}, bf16[384,3584]{1,0:T(8,128)(2,1)S(1)}, u32[]{:S(2)}, u32[]{:S(2)}) %collective-permute-start.10) | collective-permute-done | bytes 2752544 | tf_op jit(solution)/shard_map/ppermute | solution.py:14
  98.4 3.4 %convolution_convert_fusion = bf16[256,3584]{1,0:T(8,128)(2,1)S(1)} fusion(bf16[192,3584]{1,0:T(8,128)(2,1)} %copy-done.6, bf16[192,3584]{1,0:T(8,128)(2,1)S(1)} %bitcast.49, bf16[128,3584]{1,0:T(8,128)(2,1)} %slice_bitcast_fusion, f32[192,256]{1,0:T(8,128)} %get-tuple-element.19, f32[192,256]{1,0:T(8,128)} %get-tuple-element.17, ...), kind=kOutput, calls=%fused_computation | convolution fusion | flops 986578944 | bytes 6621824 | tf_op jit(solution)/shard_map/dot_general | solution.py:89
  101.9 3.5 %collective-permute-start.17 = (bf16[32,3584]{1,0:T(8,128)(2,1)S(1)}, bf16[32,3584]{1,0:T(8,128)(2,1)S(1)}, u32[]{:S(2)}, u32[]{:S(2)}) collective-permute-start(bf16[32,3584]{1,0:T(8,128)(2,1)S(1)} %get-tuple-element.12), channel_id=1, source_target_pairs={{7,0},{0,1},{1,2},{2,3},{3,4},{4,5},{5,6},{6,7},{15,8},{8,9},{9,10... | collective-permute-start | bytes 688136 | tf_op jit(solution)/shard_map/ppermute | solution.py:14
  105.4 1.9 %collective-permute-start.18 = (bf16[32,3584]{1,0:T(8,128)(2,1)S(1)}, bf16[32,3584]{1,0:T(8,128)(2,1)S(1)}, u32[]{:S(2)}, u32[]{:S(2)}) collective-permute-start(bf16[32,3584]{1,0:T(8,128)(2,1)S(1)} %get-tuple-element.11), channel_id=1, source_target_pairs={{0,2},{1,7},{2,4},{3,1},{4,6},{5,3},{6,0},{7,5},{8,10},{9,15},{10,... | collective-permute-start | bytes 688136 | tf_op jit(solution)/shard_map/ppermute | solution.py:94
  107.3 3.5 %collective-permute-start.20 = (bf16[32,3584]{1,0:T(8,128)(2,1)S(1)}, bf16[32,3584]{1,0:T(8,128)(2,1)}, u32[]{:S(2)}, u32[]{:S(2)}) collective-permute-start(bf16[32,3584]{1,0:T(8,128)(2,1)S(1)} %get-tuple-element.10), channel_id=1, source_target_pairs={{1,0},{2,1},{3,2},{4,3},{5,4},{6,5},{7,6},{0,7},{9,8},{10,9},{11,1... | collective-permute-start | bytes 688136 | tf_op jit(solution)/shard_map/ppermute | solution.py:14
  110.9 3.4 %collective-permute-start.15 = (bf16[32,3584]{1,0:T(8,128)(2,1)S(1)}, bf16[32,3584]{1,0:T(8,128)(2,1)S(1)}, u32[]{:S(2)}, u32[]{:S(2)}) collective-permute-start(bf16[32,3584]{1,0:T(8,128)(2,1)S(1)} %get-tuple-element.9), channel_id=1, source_target_pairs={{7,0},{0,1},{1,2},{2,3},{3,4},{4,5},{5,6},{6,7},{15,8},{8,9},{9,10... | collective-permute-start | bytes 688136 | tf_op jit(solution)/shard_map/ppermute | solution.py:14
  114.2 3.7 %collective-permute-start.16 = (bf16[32,3584]{1,0:T(8,128)(2,1)S(1)}, bf16[32,3584]{1,0:T(8,128)(2,1)S(1)}, u32[]{:S(2)}, u32[]{:S(2)}) collective-permute-start(bf16[32,3584]{1,0:T(8,128)(2,1)S(1)} %get-tuple-element.13), channel_id=1, source_target_pairs={{1,0},{2,1},{3,2},{4,3},{5,4},{6,5},{7,6},{0,7},{9,8},{10,9},{11,1... | collective-permute-start | bytes 688136 | tf_op jit(solution)/shard_map/ppermute | solution.py:14
  118.2 3.7 %collective-permute-done.20 = bf16[32,3584]{1,0:T(8,128)(2,1)} collective-permute-done((bf16[32,3584]{1,0:T(8,128)(2,1)S(1)}, bf16[32,3584]{1,0:T(8,128)(2,1)}, u32[]{:S(2)}, u32[]{:S(2)}) %collective-permute-start.20) | collective-permute-done | bytes 229408 | tf_op jit(solution)/shard_map/ppermute | solution.py:14
  123.0 1.9 %collective-permute-start.19 = (bf16[32,3584]{1,0:T(8,128)(2,1)S(1)}, bf16[32,3584]{1,0:T(8,128)(2,1)S(1)}, u32[]{:S(2)}, u32[]{:S(2)}) collective-permute-start(bf16[32,3584]{1,0:T(8,128)(2,1)S(1)} %get-tuple-element.7), channel_id=1, source_target_pairs={{6,0},{7,1},{0,2},{1,3},{2,4},{3,5},{4,6},{5,7},{14,8},{15,9},{8,1... | collective-permute-start | bytes 688136 | tf_op jit(solution)/shard_map/ppermute | solution.py:14
  124.9 6.0 %collective-permute-start.21 = (bf16[32,3584]{1,0:T(8,128)(2,1)S(1)}, bf16[32,3584]{1,0:T(8,128)(2,1)S(1)}, u32[]{:S(2)}, u32[]{:S(2)}) collective-permute-start(bf16[32,3584]{1,0:T(8,128)(2,1)S(1)} %get-tuple-element.8), channel_id=1, source_target_pairs={{2,0},{3,1},{4,2},{5,3},{6,4},{7,5},{0,6},{1,7},{10,8},{11,9},{12,... | collective-permute-start | bytes 688136 | tf_op jit(solution)/shard_map/ppermute | solution.py:14
  131.0 6.9 %collective-permute-done.19 = bf16[32,3584]{1,0:T(8,128)(2,1)S(1)} collective-permute-done((bf16[32,3584]{1,0:T(8,128)(2,1)S(1)}, bf16[32,3584]{1,0:T(8,128)(2,1)S(1)}, u32[]{:S(2)}, u32[]{:S(2)}) %collective-permute-start.19) | collective-permute-done | bytes 229408 | tf_op jit(solution)/shard_map/ppermute | solution.py:14
  (67 shorter events, 19.2 us)
Async XLA Ops:
  0.0 30.7 %copy-start = (bf16[128,3,3584]{2,0,1:T(8,128)(2,1)S(1)}, bf16[128,3,3584]{2,0,1:T(8,128)(2,1)}, u32[]{:S(2)}) copy-start(bf16[128,3,3584]{2,0,1:T(8,128)(2,1)} %param.9) | copy-start | bytes 8257540
  2.0 42.7 %collective-permute-start.5 = (bf16[2,32,3584]{2,1,0:T(8,128)(2,1)}, bf16[2,32,3584]{2,1,0:T(8,128)(2,1)}, u32[]{:S(2)}, u32[]{:S(2)}) collective-permute-start(bf16[2,32,3584]{2,1,0:T(8,128)(2,1)} %dynamic-slice_bitcast_fusion), channel_id=1, source_target_pairs={{8,0},{16,8},{24,16},{0,24},{9,1},{17,9},{25,17},{1,25},{10,2},{18... | collective-permute-start | bytes 1376264 | tf_op jit(solution)/shard_map/ppermute | solution.py:14
  4.4 44.0 %collective-permute-start.6 = (bf16[2,32,3584]{2,1,0:T(8,128)(2,1)}, bf16[2,32,3584]{2,1,0:T(8,128)(2,1)}, u32[]{:S(2)}, u32[]{:S(2)}) collective-permute-start(bf16[2,32,3584]{2,1,0:T(8,128)(2,1)} %dynamic-slice_bitcast_fusion), channel_id=1, source_target_pairs={{24,0},{0,8},{8,16},{16,24},{25,1},{1,9},{9,17},{17,25},{26,2},{2,... | collective-permute-start | bytes 1376264 | tf_op jit(solution)/shard_map/ppermute | solution.py:14
  7.8 44.0 %collective-permute-start.7 = (bf16[2,32,3584]{2,1,0:T(8,128)(2,1)}, bf16[2,32,3584]{2,1,0:T(8,128)(2,1)}, u32[]{:S(2)}, u32[]{:S(2)}) collective-permute-start(bf16[2,32,3584]{2,1,0:T(8,128)(2,1)} %dynamic-slice_bitcast_fusion), channel_id=1, source_target_pairs={{16,0},{24,8},{0,16},{8,24},{17,1},{25,9},{1,17},{9,25},{18,2},{26... | collective-permute-start | bytes 1376264 | tf_op jit(solution)/shard_map/ppermute | solution.py:14
  16.0 20.2 %collective-permute-start = (bf16[32,3712]{1,0:T(8,128)(2,1)S(1)}, bf16[32,3712]{1,0:T(8,128)(2,1)S(1)}, u32[]{:S(2)}, u32[]{:S(2)}) collective-permute-start(bf16[32,3712]{1,0:T(8,128)(2,1)S(1)} %concatenate.24), channel_id=1, source_target_pairs={{2,0},{3,1},{4,2},{5,3},{6,4},{7,5},{0,6},{1,7},{10,8},{11,9},{12,... | collective-permute-start | bytes 712712 | tf_op jit(solution)/shard_map/ppermute | solution.py:14
  26.9 15.5 %collective-permute-start.2 = (bf16[32,3712]{1,0:T(8,128)(2,1)S(1)}, bf16[32,3712]{1,0:T(8,128)(2,1)S(1)}, u32[]{:S(2)}, u32[]{:S(2)}) collective-permute-start(bf16[32,3712]{1,0:T(8,128)(2,1)S(1)} %concatenate.24), channel_id=1, source_target_pairs={{6,0},{7,1},{0,2},{1,3},{2,4},{3,5},{4,6},{5,7},{14,8},{15,9},{8,1... | collective-permute-start | bytes 712712 | tf_op jit(solution)/shard_map/ppermute | solution.py:14
  36.2 54.5 %collective-permute-start.4 = (bf16[32,3712]{1,0:T(8,128)(2,1)S(1)}, bf16[32,3712]{1,0:T(8,128)(2,1)S(1)}, u32[]{:S(2)}, u32[]{:S(2)}) collective-permute-start(bf16[32,3712]{1,0:T(8,128)(2,1)S(1)} %concatenate.24), channel_id=1, source_target_pairs={{4,0},{5,1},{6,2},{7,3},{0,4},{1,5},{2,6},{3,7},{12,8},{13,9},{14,... | collective-permute-start | bytes 712712 | tf_op jit(solution)/shard_map/ppermute | solution.py:14
  42.4 21.2 %collective-permute-start.11 = (bf16[2,32,3584]{2,1,0:T(8,128)(2,1)}, bf16[2,32,3584]{2,1,0:T(8,128)(2,1)S(1)}, u32[]{:S(2)}, u32[]{:S(2)}) collective-permute-start(bf16[2,32,3584]{2,1,0:T(8,128)(2,1)} %pad_maximum_fusion.7), channel_id=1, source_target_pairs={{8,0},{16,8},{24,16},{0,24},{9,1},{17,9},{25,17},{1,25},{10,2},{18... | collective-permute-start | bytes 1376264 | tf_op jit(solution)/shard_map/ppermute | solution.py:14
  44.7 24.4 %collective-permute-start.12 = (bf16[2,32,3584]{2,1,0:T(8,128)(2,1)}, bf16[2,32,3584]{2,1,0:T(8,128)(2,1)S(1)}, u32[]{:S(2)}, u32[]{:S(2)}) collective-permute-start(bf16[2,32,3584]{2,1,0:T(8,128)(2,1)} %pad_maximum_fusion.7), channel_id=1, source_target_pairs={{24,0},{0,8},{8,16},{16,24},{25,1},{1,9},{9,17},{17,25},{26,2},{2,... | collective-permute-start | bytes 1376264 | tf_op jit(solution)/shard_map/ppermute | solution.py:14
  48.4 25.4 %collective-permute-start.13 = (bf16[2,32,3584]{2,1,0:T(8,128)(2,1)}, bf16[2,32,3584]{2,1,0:T(8,128)(2,1)S(1)}, u32[]{:S(2)}, u32[]{:S(2)}) collective-permute-start(bf16[2,32,3584]{2,1,0:T(8,128)(2,1)} %pad_maximum_fusion.7), channel_id=1, source_target_pairs={{16,0},{24,8},{0,16},{8,24},{17,1},{25,9},{1,17},{9,25},{18,2},{26... | collective-permute-start | bytes 1376264 | tf_op jit(solution)/shard_map/ppermute | solution.py:14
  51.8 24.1 %collective-permute-start.1 = (bf16[64,3712]{1,0:T(8,128)(2,1)S(1)}, bf16[64,3712]{1,0:T(8,128)(2,1)S(1)}, u32[]{:S(2)}, u32[]{:S(2)}) collective-permute-start(bf16[64,3712]{1,0:T(8,128)(2,1)S(1)} %get-tuple-element.23), channel_id=1, source_target_pairs={{1,0},{2,1},{3,2},{4,3},{5,4},{6,5},{7,6},{0,7},{9,8},{10,9},{11,1... | collective-permute-start | bytes 1425416 | tf_op jit(solution)/shard_map/ppermute | solution.py:14
  55.3 22.5 %copy-start.4 = (bf16[256,3712]{1,0:T(8,128)(2,1)S(1)}, bf16[256,3712]{1,0:T(8,128)(2,1)}, u32[]{:S(2)}) copy-start(bf16[256,3712]{1,0:T(8,128)(2,1)} %constant_dynamic-update-slice_fusion.5) | copy-start | bytes 5701636
  63.7 26.9 %collective-permute-start.3 = (bf16[64,3712]{1,0:T(8,128)(2,1)S(1)}, bf16[64,3712]{1,0:T(8,128)(2,1)S(1)}, u32[]{:S(2)}, u32[]{:S(2)}) collective-permute-start(bf16[64,3712]{1,0:T(8,128)(2,1)S(1)} %get-tuple-element.22), channel_id=1, source_target_pairs={{7,0},{0,1},{1,2},{2,3},{3,4},{4,5},{5,6},{6,7},{15,8},{8,9},{9,10... | collective-permute-start | bytes 1425416 | tf_op jit(solution)/shard_map/ppermute | solution.py:14
  69.1 13.1 %collective-permute-start.8 = (bf16[96,3584]{1,0:T(8,128)(2,1)S(1)}, bf16[96,3584]{1,0:T(8,128)(2,1)S(1)}, u32[]{:S(2)}, u32[]{:S(2)}) collective-permute-start(bf16[96,3584]{1,0:T(8,128)(2,1)S(1)} %bitcast.51), channel_id=1, source_target_pairs={{448,0},{0,64},{64,128},{128,192},{192,256},{256,320},{320,384},{3... | collective-permute-start | bytes 2064392 | tf_op jit(solution)/shard_map/ppermute | solution.py:14
  73.8 14.0 %collective-permute-start.9 = (bf16[96,3584]{1,0:T(8,128)(2,1)S(1)}, bf16[96,3584]{1,0:T(8,128)(2,1)S(1)}, u32[]{:S(2)}, u32[]{:S(2)}) collective-permute-start(bf16[96,3584]{1,0:T(8,128)(2,1)S(1)} %bitcast.50), channel_id=1, source_target_pairs={{64,0},{128,64},{192,128},{256,192},{320,256},{384,320},{448,384},... | collective-permute-start | bytes 2064392 | tf_op jit(solution)/shard_map/ppermute | solution.py:14
  75.9 12.3 %copy-start.2 = (bf16[2,3,32,3584]{3,2,1,0:T(8,128)(2,1)}, bf16[2,3,32,3584]{3,2,1,0:T(8,128)(2,1)S(1)}, u32[]{:S(2)}) copy-start(bf16[2,3,32,3584]{3,2,1,0:T(8,128)(2,1)S(1)} %pad_maximum_fusion.2) | copy-start | bytes 4128772
  75.9 21.4 %collective-permute-start.14 = (bf16[192,3584]{1,0:T(8,128)(2,1)S(1)}, bf16[192,3584]{1,0:T(8,128)(2,1)S(1)}, u32[]{:S(2)}, u32[]{:S(2)}) collective-permute-start(bf16[192,3584]{1,0:T(8,128)(2,1)S(1)} %bitcast.48), channel_id=1, source_target_pairs={{32,0},{0,32},{33,1},{1,33},{34,2},{2,34},{35,3},{3,35},{36,4},{4,... | collective-permute-start | bytes 4128776 | tf_op jit(solution)/shard_map/ppermute | solution.py:14
  88.5 2.2 %copy-start.1 = (bf16[2,128,3584]{2,1,0:T(8,128)(2,1)S(1)}, bf16[2,128,3584]{2,1,0:T(8,128)(2,1)}, u32[]{:S(2)}) copy-start(bf16[2,128,3584]{2,1,0:T(8,128)(2,1)} %slice.59) | copy-start | bytes 5505028
  88.5 7.1 %collective-permute-start.10 = (bf16[384,3584]{1,0:T(8,128)(2,1)S(1)}, bf16[384,3584]{1,0:T(8,128)(2,1)S(1)}, u32[]{:S(2)}, u32[]{:S(2)}) collective-permute-start(bf16[384,3584]{1,0:T(8,128)(2,1)S(1)} %bitcast.45), channel_id=1, source_target_pairs={{32,0},{0,32},{33,1},{1,33},{34,2},{2,34},{35,3},{3,35},{36,4},{4,... | collective-permute-start | bytes 8257544 | tf_op jit(solution)/shard_map/ppermute | solution.py:14
  90.7 4.9 %copy-start.5 = (bf16[256,3712]{1,0:T(8,128)(2,1)}, bf16[256,3712]{1,0:T(8,128)(2,1)S(1)}, u32[]{:S(2)}) copy-start(bf16[256,3712]{1,0:T(8,128)(2,1)S(1)} %constant_dynamic-update-slice_fusion) | copy-start | bytes 5701636
  93.7 4.7 %copy-start.3 = (bf16[2,3,32,3584]{3,2,1,0:T(8,128)(2,1)S(1)}, bf16[2,3,32,3584]{3,2,1,0:T(8,128)(2,1)}, u32[]{:S(2)}) copy-start(bf16[2,3,32,3584]{3,2,1,0:T(8,128)(2,1)} %copy-done.2) | copy-start | bytes 4128772
  97.3 1.1 copy-start.6
  101.9 16.4 %collective-permute-start.17 = (bf16[32,3584]{1,0:T(8,128)(2,1)S(1)}, bf16[32,3584]{1,0:T(8,128)(2,1)S(1)}, u32[]{:S(2)}, u32[]{:S(2)}) collective-permute-start(bf16[32,3584]{1,0:T(8,128)(2,1)S(1)} %get-tuple-element.12), channel_id=1, source_target_pairs={{7,0},{0,1},{1,2},{2,3},{3,4},{4,5},{5,6},{6,7},{15,8},{8,9},{9,10... | collective-permute-start | bytes 688136 | tf_op jit(solution)/shard_map/ppermute | solution.py:14
  105.4 12.8 %collective-permute-start.18 = (bf16[32,3584]{1,0:T(8,128)(2,1)S(1)}, bf16[32,3584]{1,0:T(8,128)(2,1)S(1)}, u32[]{:S(2)}, u32[]{:S(2)}) collective-permute-start(bf16[32,3584]{1,0:T(8,128)(2,1)S(1)} %get-tuple-element.11), channel_id=1, source_target_pairs={{0,2},{1,7},{2,4},{3,1},{4,6},{5,3},{6,0},{7,5},{8,10},{9,15},{10,... | collective-permute-start | bytes 688136 | tf_op jit(solution)/shard_map/ppermute | solution.py:94
  107.3 14.5 %collective-permute-start.20 = (bf16[32,3584]{1,0:T(8,128)(2,1)S(1)}, bf16[32,3584]{1,0:T(8,128)(2,1)}, u32[]{:S(2)}, u32[]{:S(2)}) collective-permute-start(bf16[32,3584]{1,0:T(8,128)(2,1)S(1)} %get-tuple-element.10), channel_id=1, source_target_pairs={{1,0},{2,1},{3,2},{4,3},{5,4},{6,5},{7,6},{0,7},{9,8},{10,9},{11,1... | collective-permute-start | bytes 688136 | tf_op jit(solution)/shard_map/ppermute | solution.py:14
  110.9 20.1 %collective-permute-start.15 = (bf16[32,3584]{1,0:T(8,128)(2,1)S(1)}, bf16[32,3584]{1,0:T(8,128)(2,1)S(1)}, u32[]{:S(2)}, u32[]{:S(2)}) collective-permute-start(bf16[32,3584]{1,0:T(8,128)(2,1)S(1)} %get-tuple-element.9), channel_id=1, source_target_pairs={{7,0},{0,1},{1,2},{2,3},{3,4},{4,5},{5,6},{6,7},{15,8},{8,9},{9,10... | collective-permute-start | bytes 688136 | tf_op jit(solution)/shard_map/ppermute | solution.py:14
  114.2 16.7 %collective-permute-start.16 = (bf16[32,3584]{1,0:T(8,128)(2,1)S(1)}, bf16[32,3584]{1,0:T(8,128)(2,1)S(1)}, u32[]{:S(2)}, u32[]{:S(2)}) collective-permute-start(bf16[32,3584]{1,0:T(8,128)(2,1)S(1)} %get-tuple-element.13), channel_id=1, source_target_pairs={{1,0},{2,1},{3,2},{4,3},{5,4},{6,5},{7,6},{0,7},{9,8},{10,9},{11,1... | collective-permute-start | bytes 688136 | tf_op jit(solution)/shard_map/ppermute | solution.py:14
  123.0 14.8 %collective-permute-start.19 = (bf16[32,3584]{1,0:T(8,128)(2,1)S(1)}, bf16[32,3584]{1,0:T(8,128)(2,1)S(1)}, u32[]{:S(2)}, u32[]{:S(2)}) collective-permute-start(bf16[32,3584]{1,0:T(8,128)(2,1)S(1)} %get-tuple-element.7), channel_id=1, source_target_pairs={{6,0},{7,1},{0,2},{1,3},{2,4},{3,5},{4,6},{5,7},{14,8},{15,9},{8,1... | collective-permute-start | bytes 688136 | tf_op jit(solution)/shard_map/ppermute | solution.py:14
  124.9 14.1 %collective-permute-start.21 = (bf16[32,3584]{1,0:T(8,128)(2,1)S(1)}, bf16[32,3584]{1,0:T(8,128)(2,1)S(1)}, u32[]{:S(2)}, u32[]{:S(2)}) collective-permute-start(bf16[32,3584]{1,0:T(8,128)(2,1)S(1)} %get-tuple-element.8), channel_id=1, source_target_pairs={{2,0},{3,1},{4,2},{5,3},{6,4},{7,5},{0,6},{1,7},{10,8},{11,9},{12,... | collective-permute-start | bytes 688136 | tf_op jit(solution)/shard_map/ppermute | solution.py:14
where the time goes:
time: 141 us; the launch traced here: 140 us
  starting transfers between devices  80.3 us (57%)
  waiting for transfers between devices  35.5 us (25%)
  local copies, waits for them, and re-layouts  11.4 us (8%)
  other arithmetic  6.37 us (5%)
  matrix products  5.85 us (4%)
    ppermute x21, starting transfers between devices, from_offset(): lax.ppermute(block, axis, [((i + offset) % size, i) for i in range(size)])  78.4 us
    ppermute x21, waiting for transfers between devices, from_offset(): lax.ppermute(block, axis, [((i + offset) % size, i) for i in range(size)])  35.5 us
    dot_general x1, matrix products, returned(): lax.dot_general(hidden, rows, (((0,), (0,)), ((), ())), preferred_element...  3.39 us
  transfers between devices with their start and end apart: 22, of which 10 were waited for; matrix products, arithmetic and copies ran while one was open for 12% of the time, Pallas kernels for 0%

commit v1 on v0

--- a/solution.py
+++ b/solution.py
@@ -76,12 +76,18 @@
     return dot_t(chosen.astype(jnp.bfloat16), tail)
 
 
+def gated(product, coef):
+    rows = product.shape[0] // 2
+    gate, up = product[:rows], product[rows:]
+    return (narrow(gate / (1.0 + jnp.exp(-gate)) * up) * coef).astype(jnp.bfloat16)
+
+
 def hidden_units(coef, tokens, own, half, other):
-    first, second, third = dot_t(own, tokens), dot_t(half, tokens), dot_t(other, tokens)
-    gate = jnp.concatenate([first[:128], second[:192], third[:192]])
-    up = jnp.concatenate([first[128:], second[192:], third[192:]])
-    hidden = narrow(gate / (1.0 + jnp.exp(-gate)) * up)
-    return (hidden * coef).astype(jnp.bfloat16)
+    first = dot_t(own, tokens)
+    second, third = dot_t(half, tokens), dot_t(other, tokens)
+    return jnp.concatenate(
+        [gated(first, coef[:128]), gated(second, coef[128:320]), gated(third, coef[320:])]
+    )
 
 
 def returned(hidden, own, half, other):

time: 141 us -> 140 us (level)
  the two profiles are of different devices: /device:TPU:26 before, /device:TPU:152 now
where the time goes in v1:
time: 140 us; the launch traced here: 139 us
  starting transfers between devices  72.7 us (52%)
  waiting for transfers between devices  46.3 us (33%)
  local copies, waits for them, and re-layouts  8.9 us (6%)
  other arithmetic  6.63 us (5%)
  matrix products  4.13 us (3%)
    ppermute x21, starting transfers between devices, from_offset(): lax.ppermute(block, axis, [((i + offset) % size, i) for i in range(size)])  70.5 us
    ppermute x21, waiting for transfers between devices, from_offset(): lax.ppermute(block, axis, [((i + offset) % size, i) for i in range(size)])  46.3 us
  transfers between devices with their start and end apart: 22, of which 10 were waited for; matrix products, arithmetic and copies ran while one was open for 10% of the time, Pallas kernels for 0%

profile of v1, /device:TPU:152, one launch (start us, length us, event | category | flops | bytes accessed | tf_op | source)
XLA Modules:
  0.0 139.1 jit_solution(16636561708424929758)
XLA Ops:
  3.1 1.9 %collective-permute-start = (bf16[32,3712]{1,0:T(8,128)(2,1)S(1)}, bf16[32,3712]{1,0:T(8,128)(2,1)S(1)}, u32[]{:S(2)}, u32[]{:S(2)}) collective-permute-start(bf16[32,3712]{1,0:T(8,128)(2,1)S(1)} %concatenate.21), channel_id=1, source_target_pairs={{2,0},{3,1},{4,2},{5,3},{6,4},{7,5},{0,6},{1,7},{10,8},{11,9},{12,... | collective-permute-start | bytes 712712 | tf_op jit(solution)/shard_map/ppermute | solution.py:14
  5.0 7.3 %collective-permute-start.2 = (bf16[32,3712]{1,0:T(8,128)(2,1)S(1)}, bf16[32,3712]{1,0:T(8,128)(2,1)S(1)}, u32[]{:S(2)}, u32[]{:S(2)}) collective-permute-start(bf16[32,3712]{1,0:T(8,128)(2,1)S(1)} %concatenate.21), channel_id=1, source_target_pairs={{6,0},{7,1},{0,2},{1,3},{2,4},{3,5},{4,6},{5,7},{14,8},{15,9},{8,1... | collective-permute-start | bytes 712712 | tf_op jit(solution)/shard_map/ppermute | solution.py:14
  12.3 7.9 %collective-permute-start.4 = (bf16[32,3712]{1,0:T(8,128)(2,1)S(1)}, bf16[32,3712]{1,0:T(8,128)(2,1)}, u32[]{:S(2)}, u32[]{:S(2)}) collective-permute-start(bf16[32,3712]{1,0:T(8,128)(2,1)S(1)} %concatenate.21), channel_id=1, source_target_pairs={{4,0},{5,1},{6,2},{7,3},{0,4},{1,5},{2,6},{3,7},{12,8},{13,9},{14,... | collective-permute-start | bytes 712712 | tf_op jit(solution)/shard_map/ppermute | solution.py:14
  20.2 1.8 %dynamic-slice_bitcast_fusion = bf16[2,32,3584]{2,1,0:T(8,128)(2,1)} fusion(bf16[128,3,3584]{2,0,1:T(8,128)(2,1)} %param.9, s32[]{:T(128)S(6)} %select_n.110), kind=kLoop, calls=%fused_computation.28 | loop fusion | bytes 917508 | tf_op jit(solution)/shard_map/transpose | solution.py:46
  22.0 4.7 %collective-permute-start.5 = (bf16[2,32,3584]{2,1,0:T(8,128)(2,1)}, bf16[2,32,3584]{2,1,0:T(8,128)(2,1)}, u32[]{:S(2)}, u32[]{:S(2)}) collective-permute-start(bf16[2,32,3584]{2,1,0:T(8,128)(2,1)} %dynamic-slice_bitcast_fusion), channel_id=1, source_target_pairs={{8,0},{16,8},{24,16},{0,24},{9,1},{17,9},{25,17},{1,25},{10,2},{18... | collective-permute-start | bytes 1376264 | tf_op jit(solution)/shard_map/ppermute | solution.py:14
  26.7 1.9 %collective-permute-start.6 = (bf16[2,32,3584]{2,1,0:T(8,128)(2,1)}, bf16[2,32,3584]{2,1,0:T(8,128)(2,1)}, u32[]{:S(2)}, u32[]{:S(2)}) collective-permute-start(bf16[2,32,3584]{2,1,0:T(8,128)(2,1)} %dynamic-slice_bitcast_fusion), channel_id=1, source_target_pairs={{24,0},{0,8},{8,16},{16,24},{25,1},{1,9},{9,17},{17,25},{26,2},{2,... | collective-permute-start | bytes 1376264 | tf_op jit(solution)/shard_map/ppermute | solution.py:14
  33.6 4.2 %collective-permute-start.7 = (bf16[2,32,3584]{2,1,0:T(8,128)(2,1)}, bf16[2,32,3584]{2,1,0:T(8,128)(2,1)S(1)}, u32[]{:S(2)}, u32[]{:S(2)}) collective-permute-start(bf16[2,32,3584]{2,1,0:T(8,128)(2,1)} %dynamic-slice_bitcast_fusion), channel_id=1, source_target_pairs={{16,0},{24,8},{0,16},{8,24},{17,1},{25,9},{1,17},{9,25},{18,2},{26... | collective-permute-start | bytes 1376264 | tf_op jit(solution)/shard_map/ppermute | solution.py:14
  37.8 3.0 %collective-permute-start.11 = (bf16[2,32,3584]{2,1,0:T(8,128)(2,1)}, bf16[2,32,3584]{2,1,0:T(8,128)(2,1)S(1)}, u32[]{:S(2)}, u32[]{:S(2)}) collective-permute-start(bf16[2,32,3584]{2,1,0:T(8,128)(2,1)} %pad_maximum_fusion.5), channel_id=1, source_target_pairs={{8,0},{16,8},{24,16},{0,24},{9,1},{17,9},{25,17},{1,25},{10,2},{18... | collective-permute-start | bytes 1376264 | tf_op jit(solution)/shard_map/ppermute | solution.py:14
  41.0 2.8 %collective-permute-start.12 = (bf16[2,32,3584]{2,1,0:T(8,128)(2,1)}, bf16[2,32,3584]{2,1,0:T(8,128)(2,1)S(1)}, u32[]{:S(2)}, u32[]{:S(2)}) collective-permute-start(bf16[2,32,3584]{2,1,0:T(8,128)(2,1)} %pad_maximum_fusion.5), channel_id=1, source_target_pairs={{24,0},{0,8},{8,16},{16,24},{25,1},{1,9},{9,17},{17,25},{26,2},{2,... | collective-permute-start | bytes 1376264 | tf_op jit(solution)/shard_map/ppermute | solution.py:14
  43.8 8.1 %collective-permute-done.6 = bf16[2,32,3584]{2,1,0:T(8,128)(2,1)} collective-permute-done((bf16[2,32,3584]{2,1,0:T(8,128)(2,1)}, bf16[2,32,3584]{2,1,0:T(8,128)(2,1)}, u32[]{:S(2)}, u32[]{:S(2)}) %collective-permute-start.6) | collective-permute-done | bytes 458784 | tf_op jit(solution)/shard_map/ppermute | solution.py:14
  51.9 1.9 %collective-permute-start.13 = (bf16[2,32,3584]{2,1,0:T(8,128)(2,1)}, bf16[2,32,3584]{2,1,0:T(8,128)(2,1)S(1)}, u32[]{:S(2)}, u32[]{:S(2)}) collective-permute-start(bf16[2,32,3584]{2,1,0:T(8,128)(2,1)} %pad_maximum_fusion.5), channel_id=1, source_target_pairs={{16,0},{24,8},{0,16},{8,24},{17,1},{25,9},{1,17},{9,25},{18,2},{26... | collective-permute-start | bytes 1376264 | tf_op jit(solution)/shard_map/ppermute | solution.py:14
  53.8 1.9 %collective-permute-start.1 = (bf16[64,3712]{1,0:T(8,128)(2,1)S(1)}, bf16[64,3712]{1,0:T(8,128)(2,1)S(1)}, u32[]{:S(2)}, u32[]{:S(2)}) collective-permute-start(bf16[64,3712]{1,0:T(8,128)(2,1)S(1)} %get-tuple-element.19), channel_id=1, source_target_pairs={{1,0},{2,1},{3,2},{4,3},{5,4},{6,5},{7,6},{0,7},{9,8},{10,9},{11,1... | collective-permute-start | bytes 1425416 | tf_op jit(solution)/shard_map/ppermute | solution.py:14
  57.2 3.8 %collective-permute-done.11 = bf16[2,32,3584]{2,1,0:T(8,128)(2,1)S(1)} collective-permute-done((bf16[2,32,3584]{2,1,0:T(8,128)(2,1)}, bf16[2,32,3584]{2,1,0:T(8,128)(2,1)S(1)}, u32[]{:S(2)}, u32[]{:S(2)}) %collective-permute-start.11) | collective-permute-done | bytes 458784 | tf_op jit(solution)/shard_map/ppermute | solution.py:14
  61.0 3.4 %collective-permute-start.3 = (bf16[64,3712]{1,0:T(8,128)(2,1)S(1)}, bf16[64,3712]{1,0:T(8,128)(2,1)S(1)}, u32[]{:S(2)}, u32[]{:S(2)}) collective-permute-start(bf16[64,3712]{1,0:T(8,128)(2,1)S(1)} %get-tuple-element.18), channel_id=1, source_target_pairs={{7,0},{0,1},{1,2},{2,3},{3,4},{4,5},{5,6},{6,7},{15,8},{8,9},{9,10... | collective-permute-start | bytes 1425416 | tf_op jit(solution)/shard_map/ppermute | solution.py:14
  64.4 6.2 %collective-permute-done.12 = bf16[2,32,3584]{2,1,0:T(8,128)(2,1)S(1)} collective-permute-done((bf16[2,32,3584]{2,1,0:T(8,128)(2,1)}, bf16[2,32,3584]{2,1,0:T(8,128)(2,1)S(1)}, u32[]{:S(2)}, u32[]{:S(2)}) %collective-permute-start.12) | collective-permute-done | bytes 458784 | tf_op jit(solution)/shard_map/ppermute | solution.py:14
  70.6 4.7 %collective-permute-start.8 = (bf16[96,3584]{1,0:T(8,128)(2,1)S(1)}, bf16[96,3584]{1,0:T(8,128)(2,1)S(1)}, u32[]{:S(2)}, u32[]{:S(2)}) collective-permute-start(bf16[96,3584]{1,0:T(8,128)(2,1)S(1)} %bitcast.51), channel_id=1, source_target_pairs={{448,0},{0,64},{64,128},{128,192},{192,256},{256,320},{320,384},{3... | collective-permute-start | bytes 2064392 | tf_op jit(solution)/shard_map/ppermute | solution.py:14
  75.3 1.9 %collective-permute-start.9 = (bf16[96,3584]{1,0:T(8,128)(2,1)S(1)}, bf16[96,3584]{1,0:T(8,128)(2,1)S(1)}, u32[]{:S(2)}, u32[]{:S(2)}) collective-permute-start(bf16[96,3584]{1,0:T(8,128)(2,1)S(1)} %bitcast.50), channel_id=1, source_target_pairs={{64,0},{128,64},{192,128},{256,192},{320,256},{384,320},{448,384},... | collective-permute-start | bytes 2064392 | tf_op jit(solution)/shard_map/ppermute | solution.py:14
  77.4 1.9 %collective-permute-start.14 = (bf16[192,3584]{1,0:T(8,128)(2,1)S(1)}, bf16[192,3584]{1,0:T(8,128)(2,1)S(1)}, u32[]{:S(2)}, u32[]{:S(2)}) collective-permute-start(bf16[192,3584]{1,0:T(8,128)(2,1)S(1)} %bitcast.48), channel_id=1, source_target_pairs={{32,0},{0,32},{33,1},{1,33},{34,2},{2,34},{35,3},{3,35},{36,4},{4,... | collective-permute-start | bytes 4128776 | tf_op jit(solution)/shard_map/ppermute | solution.py:14
  79.4 4.3 %collective-permute-done.8 = bf16[96,3584]{1,0:T(8,128)(2,1)S(1)} collective-permute-done((bf16[96,3584]{1,0:T(8,128)(2,1)S(1)}, bf16[96,3584]{1,0:T(8,128)(2,1)S(1)}, u32[]{:S(2)}, u32[]{:S(2)}) %collective-permute-start.8) | collective-permute-done | bytes 688160 | tf_op jit(solution)/shard_map/ppermute | solution.py:14
  83.8 5.6 %collective-permute-done.9 = bf16[96,3584]{1,0:T(8,128)(2,1)S(1)} collective-permute-done((bf16[96,3584]{1,0:T(8,128)(2,1)S(1)}, bf16[96,3584]{1,0:T(8,128)(2,1)S(1)}, u32[]{:S(2)}, u32[]{:S(2)}) %collective-permute-start.9) | collective-permute-done | bytes 688160 | tf_op jit(solution)/shard_map/ppermute | solution.py:14
  90.0 2.1 %collective-permute-start.10 = (bf16[384,3584]{1,0:T(8,128)(2,1)S(1)}, bf16[384,3584]{1,0:T(8,128)(2,1)S(1)}, u32[]{:S(2)}, u32[]{:S(2)}) collective-permute-start(bf16[384,3584]{1,0:T(8,128)(2,1)S(1)} %bitcast.45), channel_id=1, source_target_pairs={{32,0},{0,32},{33,1},{1,33},{34,2},{2,34},{35,3},{3,35},{36,4},{4,... | collective-permute-start | bytes 8257544 | tf_op jit(solution)/shard_map/ppermute | solution.py:14
  95.1 2.0 %collective-permute-done.10 = bf16[384,3584]{1,0:T(8,128)(2,1)S(1)} collective-permute-done((bf16[384,3584]{1,0:T(8,128)(2,1)S(1)}, bf16[384,3584]{1,0:T(8,128)(2,1)S(1)}, u32[]{:S(2)}, u32[]{:S(2)}) %collective-permute-start.10) | collective-permute-done | bytes 2752544 | tf_op jit(solution)/shard_map/ppermute | solution.py:14
  99.7 3.4 %collective-permute-start.17 = (bf16[32,3584]{1,0:T(8,128)(2,1)S(1)}, bf16[32,3584]{1,0:T(8,128)(2,1)S(1)}, u32[]{:S(2)}, u32[]{:S(2)}) collective-permute-start(bf16[32,3584]{1,0:T(8,128)(2,1)S(1)} %get-tuple-element.12), channel_id=1, source_target_pairs={{7,0},{0,1},{1,2},{2,3},{3,4},{4,5},{5,6},{6,7},{15,8},{8,9},{9,10... | collective-permute-start | bytes 688136 | tf_op jit(solution)/shard_map/ppermute | solution.py:14
  103.1 2.2 %collective-permute-start.18 = (bf16[32,3584]{1,0:T(8,128)(2,1)S(1)}, bf16[32,3584]{1,0:T(8,128)(2,1)S(1)}, u32[]{:S(2)}, u32[]{:S(2)}) collective-permute-start(bf16[32,3584]{1,0:T(8,128)(2,1)S(1)} %get-tuple-element.11), channel_id=1, source_target_pairs={{0,2},{1,7},{2,4},{3,1},{4,6},{5,3},{6,0},{7,5},{8,10},{9,15},{10,... | collective-permute-start | bytes 688136 | tf_op jit(solution)/shard_map/ppermute | solution.py:100
  105.3 2.7 %collective-permute-start.20 = (bf16[32,3584]{1,0:T(8,128)(2,1)S(1)}, bf16[32,3584]{1,0:T(8,128)(2,1)}, u32[]{:S(2)}, u32[]{:S(2)}) collective-permute-start(bf16[32,3584]{1,0:T(8,128)(2,1)S(1)} %get-tuple-element.10), channel_id=1, source_target_pairs={{1,0},{2,1},{3,2},{4,3},{5,4},{6,5},{7,6},{0,7},{9,8},{10,9},{11,1... | collective-permute-start | bytes 688136 | tf_op jit(solution)/shard_map/ppermute | solution.py:14
  108.0 3.1 %collective-permute-start.15 = (bf16[32,3584]{1,0:T(8,128)(2,1)S(1)}, bf16[32,3584]{1,0:T(8,128)(2,1)S(1)}, u32[]{:S(2)}, u32[]{:S(2)}) collective-permute-start(bf16[32,3584]{1,0:T(8,128)(2,1)S(1)} %get-tuple-element.9), channel_id=1, source_target_pairs={{7,0},{0,1},{1,2},{2,3},{3,4},{4,5},{5,6},{6,7},{15,8},{8,9},{9,10... | collective-permute-start | bytes 688136 | tf_op jit(solution)/shard_map/ppermute | solution.py:14
  111.2 3.1 %collective-permute-start.16 = (bf16[32,3584]{1,0:T(8,128)(2,1)S(1)}, bf16[32,3584]{1,0:T(8,128)(2,1)S(1)}, u32[]{:S(2)}, u32[]{:S(2)}) collective-permute-start(bf16[32,3584]{1,0:T(8,128)(2,1)S(1)} %get-tuple-element.13), channel_id=1, source_target_pairs={{1,0},{2,1},{3,2},{4,3},{5,4},{6,5},{7,6},{0,7},{9,8},{10,9},{11,1... | collective-permute-start | bytes 688136 | tf_op jit(solution)/shard_map/ppermute | solution.py:14
  115.0 3.6 %collective-permute-done.20 = bf16[32,3584]{1,0:T(8,128)(2,1)} collective-permute-done((bf16[32,3584]{1,0:T(8,128)(2,1)S(1)}, bf16[32,3584]{1,0:T(8,128)(2,1)}, u32[]{:S(2)}, u32[]{:S(2)}) %collective-permute-start.20) | collective-permute-done | bytes 229408 | tf_op jit(solution)/shard_map/ppermute | solution.py:14
  119.7 4.0 %collective-permute-start.19 = (bf16[32,3584]{1,0:T(8,128)(2,1)S(1)}, bf16[32,3584]{1,0:T(8,128)(2,1)S(1)}, u32[]{:S(2)}, u32[]{:S(2)}) collective-permute-start(bf16[32,3584]{1,0:T(8,128)(2,1)S(1)} %get-tuple-element.7), channel_id=1, source_target_pairs={{6,0},{7,1},{0,2},{1,3},{2,4},{3,5},{4,6},{5,7},{14,8},{15,9},{8,1... | collective-permute-start | bytes 688136 | tf_op jit(solution)/shard_map/ppermute | solution.py:14
  123.7 2.7 %collective-permute-start.21 = (bf16[32,3584]{1,0:T(8,128)(2,1)S(1)}, bf16[32,3584]{1,0:T(8,128)(2,1)S(1)}, u32[]{:S(2)}, u32[]{:S(2)}) collective-permute-start(bf16[32,3584]{1,0:T(8,128)(2,1)S(1)} %get-tuple-element.8), channel_id=1, source_target_pairs={{2,0},{3,1},{4,2},{5,3},{6,4},{7,5},{0,6},{1,7},{10,8},{11,9},{12,... | collective-permute-start | bytes 688136 | tf_op jit(solution)/shard_map/ppermute | solution.py:14
  126.4 5.7 %collective-permute-done.19 = bf16[32,3584]{1,0:T(8,128)(2,1)S(1)} collective-permute-done((bf16[32,3584]{1,0:T(8,128)(2,1)S(1)}, bf16[32,3584]{1,0:T(8,128)(2,1)S(1)}, u32[]{:S(2)}, u32[]{:S(2)}) %collective-permute-start.19) | collective-permute-done | bytes 229408 | tf_op jit(solution)/shard_map/ppermute | solution.py:14
  132.1 6.2 %collective-permute-done.21 = bf16[32,3584]{1,0:T(8,128)(2,1)S(1)} collective-permute-done((bf16[32,3584]{1,0:T(8,128)(2,1)S(1)}, bf16[32,3584]{1,0:T(8,128)(2,1)S(1)}, u32[]{:S(2)}, u32[]{:S(2)}) %collective-permute-start.21) | collective-permute-done | bytes 229408 | tf_op jit(solution)/shard_map/ppermute | solution.py:14
  (61 shorter events, 18.6 us)
Async XLA Ops:
  0.0 30.4 %copy-start = (bf16[128,3,3584]{2,0,1:T(8,128)(2,1)S(1)}, bf16[128,3,3584]{2,0,1:T(8,128)(2,1)}, u32[]{:S(2)}) copy-start(bf16[128,3,3584]{2,0,1:T(8,128)(2,1)} %param.9) | copy-start | bytes 8257540
  3.1 30.5 %collective-permute-start = (bf16[32,3712]{1,0:T(8,128)(2,1)S(1)}, bf16[32,3712]{1,0:T(8,128)(2,1)S(1)}, u32[]{:S(2)}, u32[]{:S(2)}) collective-permute-start(bf16[32,3712]{1,0:T(8,128)(2,1)S(1)} %concatenate.21), channel_id=1, source_target_pairs={{2,0},{3,1},{4,2},{5,3},{6,4},{7,5},{0,6},{1,7},{10,8},{11,9},{12,... | collective-permute-start | bytes 712712 | tf_op jit(solution)/shard_map/ppermute | solution.py:14
  5.0 32.8 %collective-permute-start.2 = (bf16[32,3712]{1,0:T(8,128)(2,1)S(1)}, bf16[32,3712]{1,0:T(8,128)(2,1)S(1)}, u32[]{:S(2)}, u32[]{:S(2)}) collective-permute-start(bf16[32,3712]{1,0:T(8,128)(2,1)S(1)} %concatenate.21), channel_id=1, source_target_pairs={{6,0},{7,1},{0,2},{1,3},{2,4},{3,5},{4,6},{5,7},{14,8},{15,9},{8,1... | collective-permute-start | bytes 712712 | tf_op jit(solution)/shard_map/ppermute | solution.py:14
  12.3 79.9 %collective-permute-start.4 = (bf16[32,3712]{1,0:T(8,128)(2,1)S(1)}, bf16[32,3712]{1,0:T(8,128)(2,1)}, u32[]{:S(2)}, u32[]{:S(2)}) collective-permute-start(bf16[32,3712]{1,0:T(8,128)(2,1)S(1)} %concatenate.21), channel_id=1, source_target_pairs={{4,0},{5,1},{6,2},{7,3},{0,4},{1,5},{2,6},{3,7},{12,8},{13,9},{14,... | collective-permute-start | bytes 712712 | tf_op jit(solution)/shard_map/ppermute | solution.py:14
  22.0 19.0 %collective-permute-start.5 = (bf16[2,32,3584]{2,1,0:T(8,128)(2,1)}, bf16[2,32,3584]{2,1,0:T(8,128)(2,1)}, u32[]{:S(2)}, u32[]{:S(2)}) collective-permute-start(bf16[2,32,3584]{2,1,0:T(8,128)(2,1)} %dynamic-slice_bitcast_fusion), channel_id=1, source_target_pairs={{8,0},{16,8},{24,16},{0,24},{9,1},{17,9},{25,17},{1,25},{10,2},{18... | collective-permute-start | bytes 1376264 | tf_op jit(solution)/shard_map/ppermute | solution.py:14
  26.7 25.2 %collective-permute-start.6 = (bf16[2,32,3584]{2,1,0:T(8,128)(2,1)}, bf16[2,32,3584]{2,1,0:T(8,128)(2,1)}, u32[]{:S(2)}, u32[]{:S(2)}) collective-permute-start(bf16[2,32,3584]{2,1,0:T(8,128)(2,1)} %dynamic-slice_bitcast_fusion), channel_id=1, source_target_pairs={{24,0},{0,8},{8,16},{16,24},{25,1},{1,9},{9,17},{17,25},{26,2},{2,... | collective-permute-start | bytes 1376264 | tf_op jit(solution)/shard_map/ppermute | solution.py:14
  33.6 20.2 %collective-permute-start.7 = (bf16[2,32,3584]{2,1,0:T(8,128)(2,1)}, bf16[2,32,3584]{2,1,0:T(8,128)(2,1)S(1)}, u32[]{:S(2)}, u32[]{:S(2)}) collective-permute-start(bf16[2,32,3584]{2,1,0:T(8,128)(2,1)} %dynamic-slice_bitcast_fusion), channel_id=1, source_target_pairs={{16,0},{24,8},{0,16},{8,24},{17,1},{25,9},{1,17},{9,25},{18,2},{26... | collective-permute-start | bytes 1376264 | tf_op jit(solution)/shard_map/ppermute | solution.py:14
  37.8 23.2 %collective-permute-start.11 = (bf16[2,32,3584]{2,1,0:T(8,128)(2,1)}, bf16[2,32,3584]{2,1,0:T(8,128)(2,1)S(1)}, u32[]{:S(2)}, u32[]{:S(2)}) collective-permute-start(bf16[2,32,3584]{2,1,0:T(8,128)(2,1)} %pad_maximum_fusion.5), channel_id=1, source_target_pairs={{8,0},{16,8},{24,16},{0,24},{9,1},{17,9},{25,17},{1,25},{10,2},{18... | collective-permute-start | bytes 1376264 | tf_op jit(solution)/shard_map/ppermute | solution.py:14
  41.0 29.6 %collective-permute-start.12 = (bf16[2,32,3584]{2,1,0:T(8,128)(2,1)}, bf16[2,32,3584]{2,1,0:T(8,128)(2,1)S(1)}, u32[]{:S(2)}, u32[]{:S(2)}) collective-permute-start(bf16[2,32,3584]{2,1,0:T(8,128)(2,1)} %pad_maximum_fusion.5), channel_id=1, source_target_pairs={{24,0},{0,8},{8,16},{16,24},{25,1},{1,9},{9,17},{17,25},{26,2},{2,... | collective-permute-start | bytes 1376264 | tf_op jit(solution)/shard_map/ppermute | solution.py:14
  51.9 23.4 %collective-permute-start.13 = (bf16[2,32,3584]{2,1,0:T(8,128)(2,1)}, bf16[2,32,3584]{2,1,0:T(8,128)(2,1)S(1)}, u32[]{:S(2)}, u32[]{:S(2)}) collective-permute-start(bf16[2,32,3584]{2,1,0:T(8,128)(2,1)} %pad_maximum_fusion.5), channel_id=1, source_target_pairs={{16,0},{24,8},{0,16},{8,24},{17,1},{25,9},{1,17},{9,25},{18,2},{26... | collective-permute-start | bytes 1376264 | tf_op jit(solution)/shard_map/ppermute | solution.py:14
  53.8 23.6 %collective-permute-start.1 = (bf16[64,3712]{1,0:T(8,128)(2,1)S(1)}, bf16[64,3712]{1,0:T(8,128)(2,1)S(1)}, u32[]{:S(2)}, u32[]{:S(2)}) collective-permute-start(bf16[64,3712]{1,0:T(8,128)(2,1)S(1)} %get-tuple-element.19), channel_id=1, source_target_pairs={{1,0},{2,1},{3,2},{4,3},{5,4},{6,5},{7,6},{0,7},{9,8},{10,9},{11,1... | collective-permute-start | bytes 1425416 | tf_op jit(solution)/shard_map/ppermute | solution.py:14
  57.2 22.2 %copy-start.3 = (bf16[256,3712]{1,0:T(8,128)(2,1)S(1)}, bf16[256,3712]{1,0:T(8,128)(2,1)}, u32[]{:S(2)}) copy-start(bf16[256,3712]{1,0:T(8,128)(2,1)} %constant_dynamic-update-slice_fusion.5) | copy-start | bytes 5701636
  61.0 31.0 %collective-permute-start.3 = (bf16[64,3712]{1,0:T(8,128)(2,1)S(1)}, bf16[64,3712]{1,0:T(8,128)(2,1)S(1)}, u32[]{:S(2)}, u32[]{:S(2)}) collective-permute-start(bf16[64,3712]{1,0:T(8,128)(2,1)S(1)} %get-tuple-element.18), channel_id=1, source_target_pairs={{7,0},{0,1},{1,2},{2,3},{3,4},{4,5},{5,6},{6,7},{15,8},{8,9},{9,10... | collective-permute-start | bytes 1425416 | tf_op jit(solution)/shard_map/ppermute | solution.py:14
  70.6 13.1 %collective-permute-start.8 = (bf16[96,3584]{1,0:T(8,128)(2,1)S(1)}, bf16[96,3584]{1,0:T(8,128)(2,1)S(1)}, u32[]{:S(2)}, u32[]{:S(2)}) collective-permute-start(bf16[96,3584]{1,0:T(8,128)(2,1)S(1)} %bitcast.51), channel_id=1, source_target_pairs={{448,0},{0,64},{64,128},{128,192},{192,256},{256,320},{320,384},{3... | collective-permute-start | bytes 2064392 | tf_op jit(solution)/shard_map/ppermute | solution.py:14
  75.3 14.0 %collective-permute-start.9 = (bf16[96,3584]{1,0:T(8,128)(2,1)S(1)}, bf16[96,3584]{1,0:T(8,128)(2,1)S(1)}, u32[]{:S(2)}, u32[]{:S(2)}) collective-permute-start(bf16[96,3584]{1,0:T(8,128)(2,1)S(1)} %bitcast.50), channel_id=1, source_target_pairs={{64,0},{128,64},{192,128},{256,192},{320,256},{384,320},{448,384},... | collective-permute-start | bytes 2064392 | tf_op jit(solution)/shard_map/ppermute | solution.py:14
  77.4 20.8 %collective-permute-start.14 = (bf16[192,3584]{1,0:T(8,128)(2,1)S(1)}, bf16[192,3584]{1,0:T(8,128)(2,1)S(1)}, u32[]{:S(2)}, u32[]{:S(2)}) collective-permute-start(bf16[192,3584]{1,0:T(8,128)(2,1)S(1)} %bitcast.48), channel_id=1, source_target_pairs={{32,0},{0,32},{33,1},{1,33},{34,2},{2,34},{35,3},{3,35},{36,4},{4,... | collective-permute-start | bytes 4128776 | tf_op jit(solution)/shard_map/ppermute | solution.py:14
  90.0 3.2 %copy-start.1 = (bf16[2,128,3584]{2,1,0:T(8,128)(2,1)S(1)}, bf16[2,128,3584]{2,1,0:T(8,128)(2,1)}, u32[]{:S(2)}) copy-start(bf16[2,128,3584]{2,1,0:T(8,128)(2,1)} %slice.71) | copy-start | bytes 5505028
  90.0 7.1 %collective-permute-start.10 = (bf16[384,3584]{1,0:T(8,128)(2,1)S(1)}, bf16[384,3584]{1,0:T(8,128)(2,1)S(1)}, u32[]{:S(2)}, u32[]{:S(2)}) collective-permute-start(bf16[384,3584]{1,0:T(8,128)(2,1)S(1)} %bitcast.45), channel_id=1, source_target_pairs={{32,0},{0,32},{33,1},{1,33},{34,2},{2,34},{35,3},{3,35},{36,4},{4,... | collective-permute-start | bytes 8257544 | tf_op jit(solution)/shard_map/ppermute | solution.py:14
  95.1 3.1 %copy-start.2 = (bf16[128,3584]{1,0:T(8,128)(2,1)S(1)}, bf16[128,3584]{1,0:T(8,128)(2,1)}, u32[]{:S(2)}) copy-start(bf16[128,3584]{1,0:T(8,128)(2,1)} %slice_bitcast_fusion) | copy-start | bytes 2752516
  99.7 15.2 %collective-permute-start.17 = (bf16[32,3584]{1,0:T(8,128)(2,1)S(1)}, bf16[32,3584]{1,0:T(8,128)(2,1)S(1)}, u32[]{:S(2)}, u32[]{:S(2)}) collective-permute-start(bf16[32,3584]{1,0:T(8,128)(2,1)S(1)} %get-tuple-element.12), channel_id=1, source_target_pairs={{7,0},{0,1},{1,2},{2,3},{3,4},{4,5},{5,6},{6,7},{15,8},{8,9},{9,10... | collective-permute-start | bytes 688136 | tf_op jit(solution)/shard_map/ppermute | solution.py:14
  103.1 11.9 %collective-permute-start.18 = (bf16[32,3584]{1,0:T(8,128)(2,1)S(1)}, bf16[32,3584]{1,0:T(8,128)(2,1)S(1)}, u32[]{:S(2)}, u32[]{:S(2)}) collective-permute-start(bf16[32,3584]{1,0:T(8,128)(2,1)S(1)} %get-tuple-element.11), channel_id=1, source_target_pairs={{0,2},{1,7},{2,4},{3,1},{4,6},{5,3},{6,0},{7,5},{8,10},{9,15},{10,... | collective-permute-start | bytes 688136 | tf_op jit(solution)/shard_map/ppermute | solution.py:100
  105.3 13.2 %collective-permute-start.20 = (bf16[32,3584]{1,0:T(8,128)(2,1)S(1)}, bf16[32,3584]{1,0:T(8,128)(2,1)}, u32[]{:S(2)}, u32[]{:S(2)}) collective-permute-start(bf16[32,3584]{1,0:T(8,128)(2,1)S(1)} %get-tuple-element.10), channel_id=1, source_target_pairs={{1,0},{2,1},{3,2},{4,3},{5,4},{6,5},{7,6},{0,7},{9,8},{10,9},{11,1... | collective-permute-start | bytes 688136 | tf_op jit(solution)/shard_map/ppermute | solution.py:14
  108.0 18.4 %collective-permute-start.15 = (bf16[32,3584]{1,0:T(8,128)(2,1)S(1)}, bf16[32,3584]{1,0:T(8,128)(2,1)S(1)}, u32[]{:S(2)}, u32[]{:S(2)}) collective-permute-start(bf16[32,3584]{1,0:T(8,128)(2,1)S(1)} %get-tuple-element.9), channel_id=1, source_target_pairs={{7,0},{0,1},{1,2},{2,3},{3,4},{4,5},{5,6},{6,7},{15,8},{8,9},{9,10... | collective-permute-start | bytes 688136 | tf_op jit(solution)/shard_map/ppermute | solution.py:14
  111.2 15.3 %collective-permute-start.16 = (bf16[32,3584]{1,0:T(8,128)(2,1)S(1)}, bf16[32,3584]{1,0:T(8,128)(2,1)S(1)}, u32[]{:S(2)}, u32[]{:S(2)}) collective-permute-start(bf16[32,3584]{1,0:T(8,128)(2,1)S(1)} %get-tuple-element.13), channel_id=1, source_target_pairs={{1,0},{2,1},{3,2},{4,3},{5,4},{6,5},{7,6},{0,7},{9,8},{10,9},{11,1... | collective-permute-start | bytes 688136 | tf_op jit(solution)/shard_map/ppermute | solution.py:14
  119.7 12.5 %collective-permute-start.19 = (bf16[32,3584]{1,0:T(8,128)(2,1)S(1)}, bf16[32,3584]{1,0:T(8,128)(2,1)S(1)}, u32[]{:S(2)}, u32[]{:S(2)}) collective-permute-start(bf16[32,3584]{1,0:T(8,128)(2,1)S(1)} %get-tuple-element.7), channel_id=1, source_target_pairs={{6,0},{7,1},{0,2},{1,3},{2,4},{3,5},{4,6},{5,7},{14,8},{15,9},{8,1... | collective-permute-start | bytes 688136 | tf_op jit(solution)/shard_map/ppermute | solution.py:14
  123.7 14.6 %collective-permute-start.21 = (bf16[32,3584]{1,0:T(8,128)(2,1)S(1)}, bf16[32,3584]{1,0:T(8,128)(2,1)S(1)}, u32[]{:S(2)}, u32[]{:S(2)}) collective-permute-start(bf16[32,3584]{1,0:T(8,128)(2,1)S(1)} %get-tuple-element.8), channel_id=1, source_target_pairs={{2,0},{3,1},{4,2},{5,3},{6,4},{7,5},{0,6},{1,7},{10,8},{11,9},{12,... | collective-permute-start | bytes 688136 | tf_op jit(solution)/shard_map/ppermute | solution.py:14

commit v2 on v1

--- a/solution.py
+++ b/solution.py
@@ -36,8 +36,9 @@
     up2 = from_offset(own, "z", 2)
     down2 = from_offset(own, "z", -2)
     far = from_offset(own, "z", 4)
-    up13 = from_offset(jnp.concatenate([own, up2]), "z", 1)
-    down13 = from_offset(jnp.concatenate([own, down2]), "z", -1)
+    lower, upper = jnp.concatenate([own, up2]), jnp.concatenate([own, down2])
+    up13 = from_offset(lower, "z", 1)
+    down13 = from_offset(upper, "z", -1)
     return jnp.concatenate([own, up13, down13, up2, down2, far])
 
 
@@ -83,7 +84,8 @@
 
 
 def hidden_units(coef, tokens, own, half, other):
-    first = dot_t(own, tokens)
+    first = jnp.einsum("hgd,nd->ghn", own, tokens, preferred_element_type=jnp.float32)
+    first = first.reshape(256, -1)
     second, third = dot_t(half, tokens), dot_t(other, tokens)
     return jnp.concatenate(
         [gated(first, coef[:128]), gated(second, coef[128:320]), gated(third, coef[320:])]
@@ -115,14 +117,14 @@
     core, parity, x_index = lax.axis_index("core"), lax.axis_index("y") % 2, lax.axis_index("x")
     start, rest = core * 64 + parity * 32, core * 64 + 32 - parity * 32
     packed = packed_tokens(tokens, expert_ids, route_weights, owner_map)
-    planes = expert_weights.transpose(1, 0, 2)
     half, other = gate_up_pieces(expert_weights, start)
     down_half, down_other = down_pieces(expert_weights, start, rest)
     gathered = gathered_tokens(packed)
     coef = coefficients(x_index, gathered[:, width:])
-    own = planes[:2].reshape(256, width)
+    own = expert_weights[:, :2]
+    own_down = lax.optimization_barrier(expert_weights[:, 2])
     hidden = hidden_units(coef, gathered[:, :width], own, half, other)
-    return returned(hidden, planes[2], down_half, down_other).reshape(tokens.shape)
+    return returned(hidden, own_down, down_half, down_other).reshape(tokens.shape)
 
 
 def solution(mesh):

time: 140 us -> 137 us (0.979)
  waiting for transfers between devices: 46.3 us -> 42.2 us
  starting transfers between devices: 72.7 us -> 74.9 us
    ppermute x21, waiting for transfers between devices: 46.3 us -> 42.2 us  [from_offset(): lax.ppermute(block, axis, [((i + offset) % size, i) for i in range(size)])]
    ppermute x21, starting transfers between devices: 70.5 us -> 72.7 us  [from_offset(): lax.ppermute(block, axis, [((i + offset) % size, i) for i in range(size)])]
where the time goes in v2:
time: 137 us; the launch traced here: 136 us
  starting transfers between devices  74.9 us (55%)
  waiting for transfers between devices  42.2 us (31%)
  local copies, waits for them, and re-layouts  7.85 us (6%)
  other arithmetic  6.44 us (5%)
  matrix products  4.12 us (3%)
    ppermute x21, starting transfers between devices, from_offset(): lax.ppermute(block, axis, [((i + offset) % size, i) for i in range(size)])  72.7 us
    ppermute x21, waiting for transfers between devices, from_offset(): lax.ppermute(block, axis, [((i + offset) % size, i) for i in range(size)])  42.2 us
  transfers between devices with their start and end apart: 22, of which 10 were waited for; matrix products, arithmetic and copies ran while one was open for 10% of the time, Pallas kernels for 0%

profile of v2, /device:TPU:152, one launch (start us, length us, event | category | flops | bytes accessed | tf_op | source)
XLA Modules:
  0.0 136.0 jit_solution(15446926281170256030)
XLA Ops:
  3.1 1.9 %collective-permute-start = (bf16[32,3712]{1,0:T(8,128)(2,1)S(1)}, bf16[32,3712]{1,0:T(8,128)(2,1)S(1)}, u32[]{:S(2)}, u32[]{:S(2)}) collective-permute-start(bf16[32,3712]{1,0:T(8,128)(2,1)S(1)} %concatenate.21), channel_id=1, source_target_pairs={{2,0},{3,1},{4,2},{5,3},{6,4},{7,5},{0,6},{1,7},{10,8},{11,9},{12,... | collective-permute-start | bytes 712712 | tf_op jit(solution)/shard_map/ppermute | solution.py:14
  5.0 7.3 %collective-permute-start.2 = (bf16[32,3712]{1,0:T(8,128)(2,1)S(1)}, bf16[32,3712]{1,0:T(8,128)(2,1)S(1)}, u32[]{:S(2)}, u32[]{:S(2)}) collective-permute-start(bf16[32,3712]{1,0:T(8,128)(2,1)S(1)} %concatenate.21), channel_id=1, source_target_pairs={{6,0},{7,1},{0,2},{1,3},{2,4},{3,5},{4,6},{5,7},{14,8},{15,9},{8,1... | collective-permute-start | bytes 712712 | tf_op jit(solution)/shard_map/ppermute | solution.py:14
  12.3 7.9 %collective-permute-start.4 = (bf16[32,3712]{1,0:T(8,128)(2,1)S(1)}, bf16[32,3712]{1,0:T(8,128)(2,1)}, u32[]{:S(2)}, u32[]{:S(2)}) collective-permute-start(bf16[32,3712]{1,0:T(8,128)(2,1)S(1)} %concatenate.21), channel_id=1, source_target_pairs={{4,0},{5,1},{6,2},{7,3},{0,4},{1,5},{2,6},{3,7},{12,8},{13,9},{14,... | collective-permute-start | bytes 712712 | tf_op jit(solution)/shard_map/ppermute | solution.py:14
  22.0 4.9 %collective-permute-start.7 = (bf16[2,32,3584]{2,1,0:T(8,128)(2,1)}, bf16[2,32,3584]{2,1,0:T(8,128)(2,1)}, u32[]{:S(2)}, u32[]{:S(2)}) collective-permute-start(bf16[2,32,3584]{2,1,0:T(8,128)(2,1)} %dynamic-slice_bitcast_fusion), channel_id=1, source_target_pairs={{16,0},{24,8},{0,16},{8,24},{17,1},{25,9},{1,17},{9,25},{18,2},{26... | collective-permute-start | bytes 1376264 | tf_op jit(solution)/shard_map/ppermute | solution.py:14
  26.9 3.0 %collective-permute-start.5 = (bf16[2,32,3584]{2,1,0:T(8,128)(2,1)}, bf16[2,32,3584]{2,1,0:T(8,128)(2,1)}, u32[]{:S(2)}, u32[]{:S(2)}) collective-permute-start(bf16[2,32,3584]{2,1,0:T(8,128)(2,1)} %dynamic-slice_bitcast_fusion), channel_id=1, source_target_pairs={{8,0},{16,8},{24,16},{0,24},{9,1},{17,9},{25,17},{1,25},{10,2},{18... | collective-permute-start | bytes 1376264 | tf_op jit(solution)/shard_map/ppermute | solution.py:14
  30.7 2.2 %slice_bitcast_fusion = bf16[128,3584]{1,0:T(8,128)(2,1)} fusion(bf16[128,3,3584]{2,0,1:T(8,128)(2,1)} %param.9), kind=kLoop, calls=%fused_computation.19 | loop fusion | bytes 1835008 | tf_op jit(solution)/shard_map/squeeze | solution.py:125
  33.8 2.8 %collective-permute-start.6 = (bf16[2,32,3584]{2,1,0:T(8,128)(2,1)}, bf16[2,32,3584]{2,1,0:T(8,128)(2,1)S(1)}, u32[]{:S(2)}, u32[]{:S(2)}) collective-permute-start(bf16[2,32,3584]{2,1,0:T(8,128)(2,1)} %dynamic-slice_bitcast_fusion), channel_id=1, source_target_pairs={{24,0},{0,8},{8,16},{16,24},{25,1},{1,9},{9,17},{17,25},{26,2},{2,... | collective-permute-start | bytes 1376264 | tf_op jit(solution)/shard_map/ppermute | solution.py:14
  36.6 4.3 %collective-permute-start.11 = (bf16[2,32,3584]{2,1,0:T(8,128)(2,1)}, bf16[2,32,3584]{2,1,0:T(8,128)(2,1)S(1)}, u32[]{:S(2)}, u32[]{:S(2)}) collective-permute-start(bf16[2,32,3584]{2,1,0:T(8,128)(2,1)} %pad_maximum_fusion.5), channel_id=1, source_target_pairs={{8,0},{16,8},{24,16},{0,24},{9,1},{17,9},{25,17},{1,25},{10,2},{18... | collective-permute-start | bytes 1376264 | tf_op jit(solution)/shard_map/ppermute | solution.py:14
  41.0 1.9 %collective-permute-start.12 = (bf16[2,32,3584]{2,1,0:T(8,128)(2,1)}, bf16[2,32,3584]{2,1,0:T(8,128)(2,1)S(1)}, u32[]{:S(2)}, u32[]{:S(2)}) collective-permute-start(bf16[2,32,3584]{2,1,0:T(8,128)(2,1)} %pad_maximum_fusion.5), channel_id=1, source_target_pairs={{24,0},{0,8},{8,16},{16,24},{25,1},{1,9},{9,17},{17,25},{26,2},{2,... | collective-permute-start | bytes 1376264 | tf_op jit(solution)/shard_map/ppermute | solution.py:14
  42.9 6.2 %collective-permute-done.5 = bf16[2,32,3584]{2,1,0:T(8,128)(2,1)} collective-permute-done((bf16[2,32,3584]{2,1,0:T(8,128)(2,1)}, bf16[2,32,3584]{2,1,0:T(8,128)(2,1)}, u32[]{:S(2)}, u32[]{:S(2)}) %collective-permute-start.5) | collective-permute-done | bytes 458784 | tf_op jit(solution)/shard_map/ppermute | solution.py:14
  49.1 3.9 %collective-permute-start.13 = (bf16[2,32,3584]{2,1,0:T(8,128)(2,1)}, bf16[2,32,3584]{2,1,0:T(8,128)(2,1)S(1)}, u32[]{:S(2)}, u32[]{:S(2)}) collective-permute-start(bf16[2,32,3584]{2,1,0:T(8,128)(2,1)} %pad_maximum_fusion.5), channel_id=1, source_target_pairs={{16,0},{24,8},{0,16},{8,24},{17,1},{25,9},{1,17},{9,25},{18,2},{26... | collective-permute-start | bytes 1376264 | tf_op jit(solution)/shard_map/ppermute | solution.py:14
  53.0 1.9 %collective-permute-start.1 = (bf16[64,3712]{1,0:T(8,128)(2,1)S(1)}, bf16[64,3712]{1,0:T(8,128)(2,1)S(1)}, u32[]{:S(2)}, u32[]{:S(2)}) collective-permute-start(bf16[64,3712]{1,0:T(8,128)(2,1)S(1)} %get-tuple-element.19), channel_id=1, source_target_pairs={{1,0},{2,1},{3,2},{4,3},{5,4},{6,5},{7,6},{0,7},{9,8},{10,9},{11,1... | collective-permute-start | bytes 1425416 | tf_op jit(solution)/shard_map/ppermute | solution.py:14
  56.4 2.4 %collective-permute-done.11 = bf16[2,32,3584]{2,1,0:T(8,128)(2,1)S(1)} collective-permute-done((bf16[2,32,3584]{2,1,0:T(8,128)(2,1)}, bf16[2,32,3584]{2,1,0:T(8,128)(2,1)S(1)}, u32[]{:S(2)}, u32[]{:S(2)}) %collective-permute-start.11) | collective-permute-done | bytes 458784 | tf_op jit(solution)/shard_map/ppermute | solution.py:14
  58.8 3.4 %collective-permute-start.3 = (bf16[64,3712]{1,0:T(8,128)(2,1)S(1)}, bf16[64,3712]{1,0:T(8,128)(2,1)S(1)}, u32[]{:S(2)}, u32[]{:S(2)}) collective-permute-start(bf16[64,3712]{1,0:T(8,128)(2,1)S(1)} %get-tuple-element.18), channel_id=1, source_target_pairs={{7,0},{0,1},{1,2},{2,3},{3,4},{4,5},{5,6},{6,7},{15,8},{8,9},{9,10... | collective-permute-start | bytes 1425416 | tf_op jit(solution)/shard_map/ppermute | solution.py:14
  62.2 5.5 %collective-permute-done.12 = bf16[2,32,3584]{2,1,0:T(8,128)(2,1)S(1)} collective-permute-done((bf16[2,32,3584]{2,1,0:T(8,128)(2,1)}, bf16[2,32,3584]{2,1,0:T(8,128)(2,1)S(1)}, u32[]{:S(2)}, u32[]{:S(2)}) %collective-permute-start.12) | collective-permute-done | bytes 458784 | tf_op jit(solution)/shard_map/ppermute | solution.py:14
  67.6 4.7 %collective-permute-start.8 = (bf16[96,3584]{1,0:T(8,128)(2,1)S(1)}, bf16[96,3584]{1,0:T(8,128)(2,1)S(1)}, u32[]{:S(2)}, u32[]{:S(2)}) collective-permute-start(bf16[96,3584]{1,0:T(8,128)(2,1)S(1)} %bitcast.62), channel_id=1, source_target_pairs={{448,0},{0,64},{64,128},{128,192},{192,256},{256,320},{320,384},{3... | collective-permute-start | bytes 2064392 | tf_op jit(solution)/shard_map/ppermute | solution.py:14
  72.4 1.9 %collective-permute-start.9 = (bf16[96,3584]{1,0:T(8,128)(2,1)S(1)}, bf16[96,3584]{1,0:T(8,128)(2,1)S(1)}, u32[]{:S(2)}, u32[]{:S(2)}) collective-permute-start(bf16[96,3584]{1,0:T(8,128)(2,1)S(1)} %bitcast.61), channel_id=1, source_target_pairs={{64,0},{128,64},{192,128},{256,192},{320,256},{384,320},{448,384},... | collective-permute-start | bytes 2064392 | tf_op jit(solution)/shard_map/ppermute | solution.py:14
  74.4 1.9 %collective-permute-start.14 = (bf16[192,3584]{1,0:T(8,128)(2,1)S(1)}, bf16[192,3584]{1,0:T(8,128)(2,1)S(1)}, u32[]{:S(2)}, u32[]{:S(2)}) collective-permute-start(bf16[192,3584]{1,0:T(8,128)(2,1)S(1)} %bitcast.59), channel_id=1, source_target_pairs={{32,0},{0,32},{33,1},{1,33},{34,2},{2,34},{35,3},{3,35},{36,4},{4,... | collective-permute-start | bytes 4128776 | tf_op jit(solution)/shard_map/ppermute | solution.py:14
  76.4 4.3 %collective-permute-done.8 = bf16[96,3584]{1,0:T(8,128)(2,1)S(1)} collective-permute-done((bf16[96,3584]{1,0:T(8,128)(2,1)S(1)}, bf16[96,3584]{1,0:T(8,128)(2,1)S(1)}, u32[]{:S(2)}, u32[]{:S(2)}) %collective-permute-start.8) | collective-permute-done | bytes 688160 | tf_op jit(solution)/shard_map/ppermute | solution.py:14
  80.8 5.6 %collective-permute-done.9 = bf16[96,3584]{1,0:T(8,128)(2,1)S(1)} collective-permute-done((bf16[96,3584]{1,0:T(8,128)(2,1)S(1)}, bf16[96,3584]{1,0:T(8,128)(2,1)S(1)}, u32[]{:S(2)}, u32[]{:S(2)}) %collective-permute-start.9) | collective-permute-done | bytes 688160 | tf_op jit(solution)/shard_map/ppermute | solution.py:14
  87.0 1.9 %collective-permute-start.10 = (bf16[384,3584]{1,0:T(8,128)(2,1)S(1)}, bf16[384,3584]{1,0:T(8,128)(2,1)S(1)}, u32[]{:S(2)}, u32[]{:S(2)}) collective-permute-start(bf16[384,3584]{1,0:T(8,128)(2,1)S(1)} %bitcast.57), channel_id=1, source_target_pairs={{32,0},{0,32},{33,1},{1,33},{34,2},{2,34},{35,3},{3,35},{36,4},{4,... | collective-permute-start | bytes 8257544 | tf_op jit(solution)/shard_map/ppermute | solution.py:14
  92.0 2.0 %collective-permute-done.10 = bf16[384,3584]{1,0:T(8,128)(2,1)S(1)} collective-permute-done((bf16[384,3584]{1,0:T(8,128)(2,1)S(1)}, bf16[384,3584]{1,0:T(8,128)(2,1)S(1)}, u32[]{:S(2)}, u32[]{:S(2)}) %collective-permute-start.10) | collective-permute-done | bytes 2752544 | tf_op jit(solution)/shard_map/ppermute | solution.py:14
  96.6 3.4 %collective-permute-start.17 = (bf16[32,3584]{1,0:T(8,128)(2,1)S(1)}, bf16[32,3584]{1,0:T(8,128)(2,1)S(1)}, u32[]{:S(2)}, u32[]{:S(2)}) collective-permute-start(bf16[32,3584]{1,0:T(8,128)(2,1)S(1)} %get-tuple-element.12), channel_id=1, source_target_pairs={{7,0},{0,1},{1,2},{2,3},{3,4},{4,5},{5,6},{6,7},{15,8},{8,9},{9,10... | collective-permute-start | bytes 688136 | tf_op jit(solution)/shard_map/ppermute | solution.py:14
  99.9 2.2 %collective-permute-start.18 = (bf16[32,3584]{1,0:T(8,128)(2,1)S(1)}, bf16[32,3584]{1,0:T(8,128)(2,1)S(1)}, u32[]{:S(2)}, u32[]{:S(2)}) collective-permute-start(bf16[32,3584]{1,0:T(8,128)(2,1)S(1)} %get-tuple-element.11), channel_id=1, source_target_pairs={{0,2},{1,7},{2,4},{3,1},{4,6},{5,3},{6,0},{7,5},{8,10},{9,15},{10,... | collective-permute-start | bytes 688136 | tf_op jit(solution)/shard_map/ppermute | solution.py:102
  102.1 2.7 %collective-permute-start.20 = (bf16[32,3584]{1,0:T(8,128)(2,1)S(1)}, bf16[32,3584]{1,0:T(8,128)(2,1)}, u32[]{:S(2)}, u32[]{:S(2)}) collective-permute-start(bf16[32,3584]{1,0:T(8,128)(2,1)S(1)} %get-tuple-element.10), channel_id=1, source_target_pairs={{1,0},{2,1},{3,2},{4,3},{5,4},{6,5},{7,6},{0,7},{9,8},{10,9},{11,1... | collective-permute-start | bytes 688136 | tf_op jit(solution)/shard_map/ppermute | solution.py:14
  104.9 3.1 %collective-permute-start.15 = (bf16[32,3584]{1,0:T(8,128)(2,1)S(1)}, bf16[32,3584]{1,0:T(8,128)(2,1)S(1)}, u32[]{:S(2)}, u32[]{:S(2)}) collective-permute-start(bf16[32,3584]{1,0:T(8,128)(2,1)S(1)} %get-tuple-element.9), channel_id=1, source_target_pairs={{7,0},{0,1},{1,2},{2,3},{3,4},{4,5},{5,6},{6,7},{15,8},{8,9},{9,10... | collective-permute-start | bytes 688136 | tf_op jit(solution)/shard_map/ppermute | solution.py:14
  108.0 3.1 %collective-permute-start.16 = (bf16[32,3584]{1,0:T(8,128)(2,1)S(1)}, bf16[32,3584]{1,0:T(8,128)(2,1)S(1)}, u32[]{:S(2)}, u32[]{:S(2)}) collective-permute-start(bf16[32,3584]{1,0:T(8,128)(2,1)S(1)} %get-tuple-element.13), channel_id=1, source_target_pairs={{1,0},{2,1},{3,2},{4,3},{5,4},{6,5},{7,6},{0,7},{9,8},{10,9},{11,1... | collective-permute-start | bytes 688136 | tf_op jit(solution)/shard_map/ppermute | solution.py:14
  111.8 3.6 %collective-permute-done.20 = bf16[32,3584]{1,0:T(8,128)(2,1)} collective-permute-done((bf16[32,3584]{1,0:T(8,128)(2,1)S(1)}, bf16[32,3584]{1,0:T(8,128)(2,1)}, u32[]{:S(2)}, u32[]{:S(2)}) %collective-permute-start.20) | collective-permute-done | bytes 229408 | tf_op jit(solution)/shard_map/ppermute | solution.py:14
  116.5 4.0 %collective-permute-start.19 = (bf16[32,3584]{1,0:T(8,128)(2,1)S(1)}, bf16[32,3584]{1,0:T(8,128)(2,1)S(1)}, u32[]{:S(2)}, u32[]{:S(2)}) collective-permute-start(bf16[32,3584]{1,0:T(8,128)(2,1)S(1)} %get-tuple-element.7), channel_id=1, source_target_pairs={{6,0},{7,1},{0,2},{1,3},{2,4},{3,5},{4,6},{5,7},{14,8},{15,9},{8,1... | collective-permute-start | bytes 688136 | tf_op jit(solution)/shard_map/ppermute | solution.py:14
  120.5 2.7 %collective-permute-start.21 = (bf16[32,3584]{1,0:T(8,128)(2,1)S(1)}, bf16[32,3584]{1,0:T(8,128)(2,1)S(1)}, u32[]{:S(2)}, u32[]{:S(2)}) collective-permute-start(bf16[32,3584]{1,0:T(8,128)(2,1)S(1)} %get-tuple-element.8), channel_id=1, source_target_pairs={{2,0},{3,1},{4,2},{5,3},{6,4},{7,5},{0,6},{1,7},{10,8},{11,9},{12,... | collective-permute-start | bytes 688136 | tf_op jit(solution)/shard_map/ppermute | solution.py:14
  123.3 5.7 %collective-permute-done.19 = bf16[32,3584]{1,0:T(8,128)(2,1)S(1)} collective-permute-done((bf16[32,3584]{1,0:T(8,128)(2,1)S(1)}, bf16[32,3584]{1,0:T(8,128)(2,1)S(1)}, u32[]{:S(2)}, u32[]{:S(2)}) %collective-permute-start.19) | collective-permute-done | bytes 229408 | tf_op jit(solution)/shard_map/ppermute | solution.py:14
  129.0 6.2 %collective-permute-done.21 = bf16[32,3584]{1,0:T(8,128)(2,1)S(1)} collective-permute-done((bf16[32,3584]{1,0:T(8,128)(2,1)S(1)}, bf16[32,3584]{1,0:T(8,128)(2,1)S(1)}, u32[]{:S(2)}, u32[]{:S(2)}) %collective-permute-start.21) | collective-permute-done | bytes 229408 | tf_op jit(solution)/shard_map/ppermute | solution.py:14
  (58 shorter events, 16.9 us)
Async XLA Ops:
  1.8 31.1 %copy-start = (bf16[128,3,3584]{2,0,1:T(8,128)(2,1)S(1)}, bf16[128,3,3584]{2,0,1:T(8,128)(2,1)}, u32[]{:S(2)}) copy-start(bf16[128,3,3584]{2,0,1:T(8,128)(2,1)} %param.9) | copy-start | bytes 8257540
  3.1 30.7 %collective-permute-start = (bf16[32,3712]{1,0:T(8,128)(2,1)S(1)}, bf16[32,3712]{1,0:T(8,128)(2,1)S(1)}, u32[]{:S(2)}, u32[]{:S(2)}) collective-permute-start(bf16[32,3712]{1,0:T(8,128)(2,1)S(1)} %concatenate.21), channel_id=1, source_target_pairs={{2,0},{3,1},{4,2},{5,3},{6,4},{7,5},{0,6},{1,7},{10,8},{11,9},{12,... | collective-permute-start | bytes 712712 | tf_op jit(solution)/shard_map/ppermute | solution.py:14
  5.0 31.6 %collective-permute-start.2 = (bf16[32,3712]{1,0:T(8,128)(2,1)S(1)}, bf16[32,3712]{1,0:T(8,128)(2,1)S(1)}, u32[]{:S(2)}, u32[]{:S(2)}) collective-permute-start(bf16[32,3712]{1,0:T(8,128)(2,1)S(1)} %concatenate.21), channel_id=1, source_target_pairs={{6,0},{7,1},{0,2},{1,3},{2,4},{3,5},{4,6},{5,7},{14,8},{15,9},{8,1... | collective-permute-start | bytes 712712 | tf_op jit(solution)/shard_map/ppermute | solution.py:14
  12.3 76.8 %collective-permute-start.4 = (bf16[32,3712]{1,0:T(8,128)(2,1)S(1)}, bf16[32,3712]{1,0:T(8,128)(2,1)}, u32[]{:S(2)}, u32[]{:S(2)}) collective-permute-start(bf16[32,3712]{1,0:T(8,128)(2,1)S(1)} %concatenate.21), channel_id=1, source_target_pairs={{4,0},{5,1},{6,2},{7,3},{0,4},{1,5},{2,6},{3,7},{12,8},{13,9},{14,... | collective-permute-start | bytes 712712 | tf_op jit(solution)/shard_map/ppermute | solution.py:14
  22.0 19.0 %collective-permute-start.7 = (bf16[2,32,3584]{2,1,0:T(8,128)(2,1)}, bf16[2,32,3584]{2,1,0:T(8,128)(2,1)}, u32[]{:S(2)}, u32[]{:S(2)}) collective-permute-start(bf16[2,32,3584]{2,1,0:T(8,128)(2,1)} %dynamic-slice_bitcast_fusion), channel_id=1, source_target_pairs={{16,0},{24,8},{0,16},{8,24},{17,1},{25,9},{1,17},{9,25},{18,2},{26... | collective-permute-start | bytes 1376264 | tf_op jit(solution)/shard_map/ppermute | solution.py:14
  26.9 22.1 %collective-permute-start.5 = (bf16[2,32,3584]{2,1,0:T(8,128)(2,1)}, bf16[2,32,3584]{2,1,0:T(8,128)(2,1)}, u32[]{:S(2)}, u32[]{:S(2)}) collective-permute-start(bf16[2,32,3584]{2,1,0:T(8,128)(2,1)} %dynamic-slice_bitcast_fusion), channel_id=1, source_target_pairs={{8,0},{16,8},{24,16},{0,24},{9,1},{17,9},{25,17},{1,25},{10,2},{18... | collective-permute-start | bytes 1376264 | tf_op jit(solution)/shard_map/ppermute | solution.py:14
  33.8 19.2 %collective-permute-start.6 = (bf16[2,32,3584]{2,1,0:T(8,128)(2,1)}, bf16[2,32,3584]{2,1,0:T(8,128)(2,1)S(1)}, u32[]{:S(2)}, u32[]{:S(2)}) collective-permute-start(bf16[2,32,3584]{2,1,0:T(8,128)(2,1)} %dynamic-slice_bitcast_fusion), channel_id=1, source_target_pairs={{24,0},{0,8},{8,16},{16,24},{25,1},{1,9},{9,17},{17,25},{26,2},{2,... | collective-permute-start | bytes 1376264 | tf_op jit(solution)/shard_map/ppermute | solution.py:14
  36.6 22.2 %collective-permute-start.11 = (bf16[2,32,3584]{2,1,0:T(8,128)(2,1)}, bf16[2,32,3584]{2,1,0:T(8,128)(2,1)S(1)}, u32[]{:S(2)}, u32[]{:S(2)}) collective-permute-start(bf16[2,32,3584]{2,1,0:T(8,128)(2,1)} %pad_maximum_fusion.5), channel_id=1, source_target_pairs={{8,0},{16,8},{24,16},{0,24},{9,1},{17,9},{25,17},{1,25},{10,2},{18... | collective-permute-start | bytes 1376264 | tf_op jit(solution)/shard_map/ppermute | solution.py:14
  41.0 26.7 %collective-permute-start.12 = (bf16[2,32,3584]{2,1,0:T(8,128)(2,1)}, bf16[2,32,3584]{2,1,0:T(8,128)(2,1)S(1)}, u32[]{:S(2)}, u32[]{:S(2)}) collective-permute-start(bf16[2,32,3584]{2,1,0:T(8,128)(2,1)} %pad_maximum_fusion.5), channel_id=1, source_target_pairs={{24,0},{0,8},{8,16},{16,24},{25,1},{1,9},{9,17},{17,25},{26,2},{2,... | collective-permute-start | bytes 1376264 | tf_op jit(solution)/shard_map/ppermute | solution.py:14
  49.1 23.3 %collective-permute-start.13 = (bf16[2,32,3584]{2,1,0:T(8,128)(2,1)}, bf16[2,32,3584]{2,1,0:T(8,128)(2,1)S(1)}, u32[]{:S(2)}, u32[]{:S(2)}) collective-permute-start(bf16[2,32,3584]{2,1,0:T(8,128)(2,1)} %pad_maximum_fusion.5), channel_id=1, source_target_pairs={{16,0},{24,8},{0,16},{8,24},{17,1},{25,9},{1,17},{9,25},{18,2},{26... | collective-permute-start | bytes 1376264 | tf_op jit(solution)/shard_map/ppermute | solution.py:14
  53.0 21.4 %collective-permute-start.1 = (bf16[64,3712]{1,0:T(8,128)(2,1)S(1)}, bf16[64,3712]{1,0:T(8,128)(2,1)S(1)}, u32[]{:S(2)}, u32[]{:S(2)}) collective-permute-start(bf16[64,3712]{1,0:T(8,128)(2,1)S(1)} %get-tuple-element.19), channel_id=1, source_target_pairs={{1,0},{2,1},{3,2},{4,3},{5,4},{6,5},{7,6},{0,7},{9,8},{10,9},{11,1... | collective-permute-start | bytes 1425416 | tf_op jit(solution)/shard_map/ppermute | solution.py:14
  56.3 20.0 %copy-start.2 = (bf16[256,3712]{1,0:T(8,128)(2,1)S(1)}, bf16[256,3712]{1,0:T(8,128)(2,1)}, u32[]{:S(2)}) copy-start(bf16[256,3712]{1,0:T(8,128)(2,1)} %constant_dynamic-update-slice_fusion.5) | copy-start | bytes 5701636
  58.8 30.1 %collective-permute-start.3 = (bf16[64,3712]{1,0:T(8,128)(2,1)S(1)}, bf16[64,3712]{1,0:T(8,128)(2,1)S(1)}, u32[]{:S(2)}, u32[]{:S(2)}) collective-permute-start(bf16[64,3712]{1,0:T(8,128)(2,1)S(1)} %get-tuple-element.18), channel_id=1, source_target_pairs={{7,0},{0,1},{1,2},{2,3},{3,4},{4,5},{5,6},{6,7},{15,8},{8,9},{9,10... | collective-permute-start | bytes 1425416 | tf_op jit(solution)/shard_map/ppermute | solution.py:14
  67.6 13.1 %collective-permute-start.8 = (bf16[96,3584]{1,0:T(8,128)(2,1)S(1)}, bf16[96,3584]{1,0:T(8,128)(2,1)S(1)}, u32[]{:S(2)}, u32[]{:S(2)}) collective-permute-start(bf16[96,3584]{1,0:T(8,128)(2,1)S(1)} %bitcast.62), channel_id=1, source_target_pairs={{448,0},{0,64},{64,128},{128,192},{192,256},{256,320},{320,384},{3... | collective-permute-start | bytes 2064392 | tf_op jit(solution)/shard_map/ppermute | solution.py:14
  72.4 14.0 %collective-permute-start.9 = (bf16[96,3584]{1,0:T(8,128)(2,1)S(1)}, bf16[96,3584]{1,0:T(8,128)(2,1)S(1)}, u32[]{:S(2)}, u32[]{:S(2)}) collective-permute-start(bf16[96,3584]{1,0:T(8,128)(2,1)S(1)} %bitcast.61), channel_id=1, source_target_pairs={{64,0},{128,64},{192,128},{256,192},{320,256},{384,320},{448,384},... | collective-permute-start | bytes 2064392 | tf_op jit(solution)/shard_map/ppermute | solution.py:14
  74.4 20.6 %collective-permute-start.14 = (bf16[192,3584]{1,0:T(8,128)(2,1)S(1)}, bf16[192,3584]{1,0:T(8,128)(2,1)S(1)}, u32[]{:S(2)}, u32[]{:S(2)}) collective-permute-start(bf16[192,3584]{1,0:T(8,128)(2,1)S(1)} %bitcast.59), channel_id=1, source_target_pairs={{32,0},{0,32},{33,1},{1,33},{34,2},{2,34},{35,3},{3,35},{36,4},{4,... | collective-permute-start | bytes 4128776 | tf_op jit(solution)/shard_map/ppermute | solution.py:14
  87.0 7.0 %collective-permute-start.10 = (bf16[384,3584]{1,0:T(8,128)(2,1)S(1)}, bf16[384,3584]{1,0:T(8,128)(2,1)S(1)}, u32[]{:S(2)}, u32[]{:S(2)}) collective-permute-start(bf16[384,3584]{1,0:T(8,128)(2,1)S(1)} %bitcast.57), channel_id=1, source_target_pairs={{32,0},{0,32},{33,1},{1,33},{34,2},{2,34},{35,3},{3,35},{36,4},{4,... | collective-permute-start | bytes 8257544 | tf_op jit(solution)/shard_map/ppermute | solution.py:14
  92.0 3.1 %copy-start.1 = (bf16[128,3584]{1,0:T(8,128)(2,1)S(1)}, bf16[128,3584]{1,0:T(8,128)(2,1)}, u32[]{:S(2)}) copy-start(bf16[128,3584]{1,0:T(8,128)(2,1)} %slice_bitcast_fusion) | copy-start | bytes 2752516
  96.6 15.2 %collective-permute-start.17 = (bf16[32,3584]{1,0:T(8,128)(2,1)S(1)}, bf16[32,3584]{1,0:T(8,128)(2,1)S(1)}, u32[]{:S(2)}, u32[]{:S(2)}) collective-permute-start(bf16[32,3584]{1,0:T(8,128)(2,1)S(1)} %get-tuple-element.12), channel_id=1, source_target_pairs={{7,0},{0,1},{1,2},{2,3},{3,4},{4,5},{5,6},{6,7},{15,8},{8,9},{9,10... | collective-permute-start | bytes 688136 | tf_op jit(solution)/shard_map/ppermute | solution.py:14
  99.9 11.9 %collective-permute-start.18 = (bf16[32,3584]{1,0:T(8,128)(2,1)S(1)}, bf16[32,3584]{1,0:T(8,128)(2,1)S(1)}, u32[]{:S(2)}, u32[]{:S(2)}) collective-permute-start(bf16[32,3584]{1,0:T(8,128)(2,1)S(1)} %get-tuple-element.11), channel_id=1, source_target_pairs={{0,2},{1,7},{2,4},{3,1},{4,6},{5,3},{6,0},{7,5},{8,10},{9,15},{10,... | collective-permute-start | bytes 688136 | tf_op jit(solution)/shard_map/ppermute | solution.py:102
  102.1 13.2 %collective-permute-start.20 = (bf16[32,3584]{1,0:T(8,128)(2,1)S(1)}, bf16[32,3584]{1,0:T(8,128)(2,1)}, u32[]{:S(2)}, u32[]{:S(2)}) collective-permute-start(bf16[32,3584]{1,0:T(8,128)(2,1)S(1)} %get-tuple-element.10), channel_id=1, source_target_pairs={{1,0},{2,1},{3,2},{4,3},{5,4},{6,5},{7,6},{0,7},{9,8},{10,9},{11,1... | collective-permute-start | bytes 688136 | tf_op jit(solution)/shard_map/ppermute | solution.py:14
  104.9 18.4 %collective-permute-start.15 = (bf16[32,3584]{1,0:T(8,128)(2,1)S(1)}, bf16[32,3584]{1,0:T(8,128)(2,1)S(1)}, u32[]{:S(2)}, u32[]{:S(2)}) collective-permute-start(bf16[32,3584]{1,0:T(8,128)(2,1)S(1)} %get-tuple-element.9), channel_id=1, source_target_pairs={{7,0},{0,1},{1,2},{2,3},{3,4},{4,5},{5,6},{6,7},{15,8},{8,9},{9,10... | collective-permute-start | bytes 688136 | tf_op jit(solution)/shard_map/ppermute | solution.py:14
  108.0 15.2 %collective-permute-start.16 = (bf16[32,3584]{1,0:T(8,128)(2,1)S(1)}, bf16[32,3584]{1,0:T(8,128)(2,1)S(1)}, u32[]{:S(2)}, u32[]{:S(2)}) collective-permute-start(bf16[32,3584]{1,0:T(8,128)(2,1)S(1)} %get-tuple-element.13), channel_id=1, source_target_pairs={{1,0},{2,1},{3,2},{4,3},{5,4},{6,5},{7,6},{0,7},{9,8},{10,9},{11,1... | collective-permute-start | bytes 688136 | tf_op jit(solution)/shard_map/ppermute | solution.py:14
  116.5 12.5 %collective-permute-start.19 = (bf16[32,3584]{1,0:T(8,128)(2,1)S(1)}, bf16[32,3584]{1,0:T(8,128)(2,1)S(1)}, u32[]{:S(2)}, u32[]{:S(2)}) collective-permute-start(bf16[32,3584]{1,0:T(8,128)(2,1)S(1)} %get-tuple-element.7), channel_id=1, source_target_pairs={{6,0},{7,1},{0,2},{1,3},{2,4},{3,5},{4,6},{5,7},{14,8},{15,9},{8,1... | collective-permute-start | bytes 688136 | tf_op jit(solution)/shard_map/ppermute | solution.py:14
  120.5 14.7 %collective-permute-start.21 = (bf16[32,3584]{1,0:T(8,128)(2,1)S(1)}, bf16[32,3584]{1,0:T(8,128)(2,1)S(1)}, u32[]{:S(2)}, u32[]{:S(2)}) collective-permute-start(bf16[32,3584]{1,0:T(8,128)(2,1)S(1)} %get-tuple-element.8), channel_id=1, source_target_pairs={{2,0},{3,1},{4,2},{5,3},{6,4},{7,5},{0,6},{1,7},{10,8},{11,9},{12,... | collective-permute-start | bytes 688136 | tf_op jit(solution)/shard_map/ppermute | solution.py:14
